TPU v7x, 32 devices: a whole 2x2x4 slice. The times are simulated.
32 devices in a mesh: dp: 2 (over core), row: 4 (over y, x), col: 4 (over z).
Axes of the slice: x: 2, y: 2, z: 4, core: 2. Of those that a mesh axis runs over, the one named last changes fastest.
Arguments:
- block_input: bfloat16 [768, 8192], P('row', ('dp', 'col')), may hold values from -6 to 6
- norm_gains: float32 [2, 768], P(None, 'row'), may hold values from 0.1 to 1.9
- row_biases: float32 [4, 768], P(None, 'row'), may hold values from -3 to 3
- w_qkv: bfloat16 [768, 3, 768], P('row', None, 'col'), may hold values from -0.21875 to 0.21875
- qv_bias: float32 [2, 768], P(None, 'col'), may hold values from -3 to 3
- w_out: bfloat16 [768, 768], P('col', 'row'), may hold values from -0.625 to 0.625
- w_up: bfloat16 [768, 3072], P('row', 'col'), may hold values from -0.21875 to 0.21875
- up_bias: float32 [3072], P('col'), may hold values from -3 to 3
- w_down: bfloat16 [768, 3072], P('row', 'col'), may hold values from -0.15625 to 0.15625
- cotangent: bfloat16 [768, 8192], P('row', ('dp', 'col')), may hold values from -6 to 6
Outputs:
- block_output: bfloat16 [768, 8192], P('row', ('dp', 'col'))
- grad_x: bfloat16 [768, 8192], P('row', ('dp', 'col'))
- grad_norm_gains: float32 [2, 768], P(None, 'row')
- grad_row_biases: float32 [4, 768], P(None, 'row')
- grad_w_qkv: float32 [768, 3, 768], P('row', None, 'col')
- grad_qv_bias: float32 [2, 768], P(None, 'col')
- grad_w_out: float32 [768, 768], P('col', 'row')
- grad_w_up: float32 [768, 3072], P('row', 'col')
- grad_up_bias: float32 [3072], P('col')
- grad_w_down: float32 [768, 3072], P('row', 'col')
All inputs are finite; a program needn't handle non-finite values.
Results may differ from a plain program's by a relative error of at most 0.013.
Values may be sent and summed in bfloat16 or wider, within the bound.
A program may use at most 192 MiB of HBM per device.

v0:
```python
import jax
import jax.numpy as jnp
from jax import lax
from jax.sharding import PartitionSpec as P

D = 768
HEAD = 64
LENGTH = 512


EPSILON = 1e-05
GELU_COEF = 0.7978845608028654


def gelu_tanh(values):
    return (
        0.5 * values * (1.0 + jnp.tanh(GELU_COEF * (values + 0.044715 * values * values * values)))
    )


def multiply(rows, weight, flipped):
    if flipped:
        return lax.dot_general(
            rows, weight, (((1,), (1,)), ((), ())), preferred_element_type=jnp.float32
        )
    return jnp.dot(rows, weight, preferred_element_type=jnp.float32)


def contract_tokens(left, right):
    return lax.dot_general(
        left, right, (((0,), (0,)), ((), ())), preferred_element_type=jnp.float32
    )


def across_cols(local, weight, flipped):
    gathered = lax.all_gather(local, "col", axis=0, tiled=True)
    share = gathered.shape[0] // lax.axis_size("row")

    def partial_rows(start, count):
        return multiply(gathered, weight, flipped)

    return (
        gathered,
        lax.psum_scatter(
            partial_rows(jnp.int32(0), lax.axis_size("row") * share),
            "row",
            scatter_dimension=0,
            tiled=True,
        ),
    )


def across_rows(local, weight, flipped):
    gathered = lax.all_gather(local, "row", axis=0, tiled=True)
    share = gathered.shape[0] // lax.axis_size("col")

    def partial_rows(start, count):
        return multiply(gathered, weight, flipped)

    return (
        gathered,
        lax.psum_scatter(
            partial_rows(jnp.int32(0), lax.axis_size("col") * share),
            "col",
            scatter_dimension=0,
            tiled=True,
        ),
    )


def regather_cols(local):
    return lax.all_gather(local, "col", axis=0, tiled=True)


def regather_rows(local):
    return lax.all_gather(local, "row", axis=0, tiled=True)


def norm_forward(values, gain, bias):
    center = lax.psum(jnp.sum(values, axis=1), "row") / D
    offset = values - center[:, None]
    spread = lax.psum(jnp.sum(offset * offset, axis=1), "row") / D
    inverse = lax.rsqrt(spread + EPSILON)
    normal = offset * inverse[:, None]
    return (normal * gain + bias, normal, inverse)


def norm_backward(grad, gain, normal, inverse):
    scaled = grad * gain
    first, second = lax.psum((jnp.sum(scaled, axis=1), jnp.sum(scaled * normal, axis=1)), "row")
    result = inverse[:, None] * (scaled - first[:, None] / D - normal * (second[:, None] / D))
    return (result, jnp.sum(grad * normal, axis=0), jnp.sum(grad, axis=0))


def causal_mask(length):
    positions = jnp.arange(length)
    return positions[None, :] <= positions[:, None]


def attention_forward(queries, keys, values):
    factor = HEAD ** (-0.5)

    def one_sequence(pieces):
        seq_q, seq_k, seq_v = pieces
        scores = (
            jnp.einsum("qhd,khd->hqk", seq_q, seq_k, preferred_element_type=jnp.float32) * factor
        )
        scores = jnp.where(causal_mask(seq_q.shape[0])[None], scores, -1e30)
        summit = jnp.max(scores, axis=-1, keepdims=True)
        expos = jnp.exp(scores - summit)
        total = jnp.sum(expos, axis=-1, keepdims=True)
        probs = (expos / total).astype(jnp.bfloat16)
        output = jnp.einsum("hqk,khd->qhd", probs, seq_v, preferred_element_type=jnp.float32)
        return (output, summit[..., 0] + jnp.log(total[..., 0]))

    return lax.map(one_sequence, (queries, keys, values))


def attention_backward(queries, keys, values, grad_out, log_sums):
    factor = HEAD ** (-0.5)

    def one_sequence(pieces):
        seq_q, seq_k, seq_v, seq_g, seq_l = pieces
        scores = (
            jnp.einsum("qhd,khd->hqk", seq_q, seq_k, preferred_element_type=jnp.float32) * factor
        )
        scores = jnp.where(causal_mask(seq_q.shape[0])[None], scores, -1e30)
        probs = jnp.exp(scores - seq_l[..., None])
        grad_v = jnp.einsum(
            "hqk,qhd->khd", probs.astype(jnp.bfloat16), seq_g, preferred_element_type=jnp.float32
        )
        grad_p = jnp.einsum("qhd,khd->hqk", seq_g, seq_v, preferred_element_type=jnp.float32)
        inner = jnp.sum(grad_p * probs, axis=-1, keepdims=True)
        grad_s = (probs * (grad_p - inner)).astype(jnp.bfloat16)
        grad_q = (
            jnp.einsum("hqk,khd->qhd", grad_s, seq_k, preferred_element_type=jnp.float32) * factor
        )
        grad_k = (
            jnp.einsum("hqk,qhd->khd", grad_s, seq_q, preferred_element_type=jnp.float32) * factor
        )
        return (grad_q, grad_k, grad_v)

    return lax.map(one_sequence, (queries, keys, values, grad_out, log_sums))


def body(
    block_input, norm_gains, row_biases, w_qkv, qv_bias, w_out, w_up, up_bias, w_down, cotangent
):
    inputs = block_input.T.astype(jnp.float32)
    cot_rows = cotangent.T
    normed_one, normal_one, inverse_one = norm_forward(inputs, norm_gains[0], row_biases[0])
    normed_one_low = normed_one.astype(jnp.bfloat16)
    qkv_weight = w_qkv.reshape(w_qkv.shape[0], -1)
    gathered_one, qkv_sum = across_cols(normed_one_low, qkv_weight, False)
    rows_here = qkv_sum.shape[0]
    head_cols = w_qkv.shape[2]
    qkv_sum = qkv_sum.reshape(rows_here, 3, head_cols)
    shape_four = (rows_here // LENGTH, LENGTH, head_cols // HEAD, HEAD)
    queries = (qkv_sum[:, 0] + qv_bias[0]).astype(jnp.bfloat16).reshape(shape_four)
    keys_all = qkv_sum[:, 1].astype(jnp.bfloat16).reshape(shape_four)
    values_all = (qkv_sum[:, 2] + qv_bias[1]).astype(jnp.bfloat16).reshape(shape_four)
    attended, log_sums = attention_forward(queries, keys_all, values_all)
    attended_low = attended.reshape(rows_here, head_cols).astype(jnp.bfloat16)
    gathered_att, projected = across_rows(attended_low, w_out, False)
    middle = inputs + projected + row_biases[2]
    normed_two, normal_two, inverse_two = norm_forward(middle, norm_gains[1], row_biases[1])
    normed_two_low = normed_two.astype(jnp.bfloat16)
    gathered_two, up_sum = across_cols(normed_two_low, w_up, False)
    before = up_sum + up_bias
    hidden_low = gelu_tanh(before).astype(jnp.bfloat16)
    gathered_hid, down_sum = across_rows(hidden_low, w_down, True)
    output = middle + down_sum + row_biases[3]
    source_one = regather_cols(normed_one_low)
    source_two = regather_cols(normed_two_low)
    source_att = regather_rows(attended_low)
    source_hid = regather_rows(hidden_low)
    grad_out = cot_rows.astype(jnp.float32)
    gathered_dy, grad_hidden = across_cols(cot_rows, w_down, False)
    grad_w_down = contract_tokens(gathered_dy, source_hid)
    pull_gelu = jax.vjp(gelu_tanh, before)[1]
    grad_before = pull_gelu(grad_hidden)[0].astype(jnp.bfloat16)
    grad_up_bias = jnp.sum(grad_before.astype(jnp.float32), axis=0)
    gathered_du, grad_normed_two = across_rows(grad_before, w_up, True)
    grad_w_up = contract_tokens(source_two, gathered_du)
    back_two, gain_two, shift_two = norm_backward(
        grad_normed_two, norm_gains[1], normal_two, inverse_two
    )
    grad_middle = grad_out + back_two
    grad_middle_low = grad_middle.astype(jnp.bfloat16)
    grad_out_bias = jnp.sum(grad_middle_low.astype(jnp.float32), axis=0)
    grad_down_bias = jnp.sum(grad_out, axis=0)
    gathered_dm, grad_attended = across_cols(grad_middle_low, w_out, True)
    grad_w_out = contract_tokens(source_att, gathered_dm)
    grad_att_low = grad_attended.astype(jnp.bfloat16).reshape(shape_four)
    grad_q, grad_k, grad_v = attention_backward(
        queries, keys_all, values_all, grad_att_low, log_sums
    )
    grad_q = grad_q.reshape(rows_here, head_cols).astype(jnp.bfloat16)
    grad_k = grad_k.reshape(rows_here, head_cols).astype(jnp.bfloat16)
    grad_v = grad_v.reshape(rows_here, head_cols).astype(jnp.bfloat16)
    grad_qkv_low = jnp.stack([grad_q, grad_k, grad_v], axis=1).reshape(rows_here, 3 * head_cols)
    grad_qv = jnp.stack(
        [jnp.sum(grad_q.astype(jnp.float32), axis=0), jnp.sum(grad_v.astype(jnp.float32), axis=0)]
    )
    gathered_dqkv, grad_normed_one = across_rows(grad_qkv_low, qkv_weight, True)
    grad_w_qkv = contract_tokens(source_one, gathered_dqkv).reshape(w_qkv.shape)
    back_one, gain_one, shift_one = norm_backward(
        grad_normed_one, norm_gains[0], normal_one, inverse_one
    )
    grad_input = grad_middle + back_one
    sum_qkv, sum_out, sum_up, sum_down = (
        lax.psum(grad_w_qkv.astype(jnp.bfloat16), "dp").astype(jnp.float32),
        lax.psum(grad_w_out.astype(jnp.bfloat16), "dp").astype(jnp.float32),
        lax.psum(grad_w_up.astype(jnp.bfloat16), "dp").astype(jnp.float32),
        lax.psum(grad_w_down.astype(jnp.bfloat16), "dp").astype(jnp.float32),
    )
    gain_grads = jnp.stack([gain_one, gain_two])
    shift_grads = jnp.stack([shift_one, shift_two, grad_out_bias, grad_down_bias])
    sum_gains, sum_shifts = lax.psum((gain_grads, shift_grads), ("dp", "col"))
    sum_qv, sum_upb = lax.psum((grad_qv, grad_up_bias), ("dp", "row"))
    return (
        output.astype(jnp.bfloat16).T,
        grad_input.astype(jnp.bfloat16).T,
        sum_gains,
        sum_shifts,
        sum_qkv,
        sum_qv,
        sum_out,
        sum_up,
        sum_upb,
        sum_down,
    )


def solution(mesh):
    in_specs = (
        P("row", ("dp", "col")),
        P(None, "row"),
        P(None, "row"),
        P("row", None, "col"),
        P(None, "col"),
        P("col", "row"),
        P("row", "col"),
        P("col"),
        P("row", "col"),
        P("row", ("dp", "col")),
    )
    out_specs = (
        P("row", ("dp", "col")),
        P("row", ("dp", "col")),
        P(None, "row"),
        P(None, "row"),
        P("row", None, "col"),
        P(None, "col"),
        P("col", "row"),
        P("row", "col"),
        P("col"),
        P("row", "col"),
    )
    return jax.shard_map(body, mesh=mesh, in_specs=in_specs, out_specs=out_specs, check_vma=False)
```

profile of v0, /device:TPU:2, one launch (start us, length us, event | category | flops | bytes accessed | tf_op | source)
XLA Modules:
  0.0 1146.0 jit_solution(9692835107148929865)
XLA Ops:
  7.2 1.1 convert_reduce_fusion.2
  8.3 8.1 psum.112
  16.4 1.1 fusion.71
  17.5 9.8 psum.113
  29.0 1.9 fusion.64
  31.0 1.1 copy.30
  32.1 36.3 %all-gather.9.cloned.1.call-done = bf16[4096,192]{0,1:T(8,128)(2,1)} async-done(((bf16[1024,192]{0,1:T(8,128)(2,1)}), bf16[4096,192]{0,1:T(8,128)(2,1)}) %all-gather.9.cloned.1.call-update) | async-done | bytes 1572880 | tf_op jit(solution)/shard_map/all_gather | solution.py:36
  68.4 6.4 fusion.89
  75.7 93.1 %reduce-scatter.9.cloned.1.call-done = f32[1024,576]{0,1:T(8,128)} async-done(((f32[4096,576]{0,1:T(8,128)}), f32[1024,576]{0,1:T(8,128)}) %reduce-scatter.9.cloned.1.call-update) | async-done | bytes 2359312 | tf_op jit(solution)/shard_map/reduce_scatter | solution.py:44
  168.8 1.5 fusion.80
  170.3 1.2 slice.53
  174.0 5.4 while.26
  175.6 1.1 fusion.135
  178.3 1.1 fusion.135
  180.7 30.9 %all-gather.11.cloned.1.call-done = bf16[4096,192]{0,1:T(8,128)(2,1)} async-done(((bf16[1024,192]{0,1:T(8,128)(2,1)}), bf16[4096,192]{0,1:T(8,128)(2,1)}) %all-gather.11.cloned.1.call-update) | async-done | bytes 1572880 | tf_op jit(solution)/shard_map/all_gather | solution.py:54
  211.7 3.7 fusion.83
  216.0 59.9 %reduce-scatter.11.cloned.1.call-done = f32[1024,192]{0,1:T(8,128)} async-done(((f32[4096,192]{0,1:T(8,128)}), f32[1024,192]{0,1:T(8,128)}) %reduce-scatter.11.cloned.1.call-update) | async-done | bytes 786448 | tf_op jit(solution)/shard_map/reduce_scatter | solution.py:62
  275.9 1.3 fusion.78
  277.2 8.1 psum.114
  285.4 9.8 psum.115
  296.2 18.1 %all-gather.17.cloned.1.call-done = bf16[4096,192]{0,1:T(8,128)(2,1)} async-done(((bf16[1024,192]{0,1:T(8,128)(2,1)}), bf16[4096,192]{0,1:T(8,128)(2,1)}) %all-gather.17.cloned.1.call-update) | async-done | bytes 1572880 | tf_op jit(solution)/shard_map/all_gather | solution.py:36
  314.3 7.8 fusion.86
  322.4 29.8 %all-gather.13.cloned.1.call-done = bf16[4096,192]{0,1:T(8,128)(2,1)} async-done(((bf16[1024,192]{0,1:T(8,128)(2,1)}), bf16[4096,192]{0,1:T(8,128)(2,1)}) %all-gather.13.cloned.1.call-update) | async-done | bytes 1572880 | tf_op jit(solution)/shard_map/all_gather | solution.py:36
  352.2 7.7 fusion.84
  360.1 114.8 %reduce-scatter.17.cloned.1.call-done = f32[1024,768]{1,0:T(8,128)} async-done(((f32[4096,768]{1,0:T(8,128)}), f32[1024,768]{1,0:T(8,128)}) %reduce-scatter.17.cloned.1.call-update) | async-done | bytes 3145744 | tf_op jit(solution)/shard_map/reduce_scatter | solution.py:44
  474.8 123.7 %reduce-scatter.13.cloned.1.call-done = f32[1024,768]{1,0:T(8,128)} async-done(((f32[4096,768]{1,0:T(8,128)}), f32[1024,768]{1,0:T(8,128)}) %reduce-scatter.13.cloned.1.call-update) | async-done | bytes 3145744 | tf_op jit(solution)/shard_map/reduce_scatter | solution.py:44
  598.6 6.2 convert_reduce_fusion
  604.9 70.1 %all-gather.19.cloned.1.call-done = bf16[4096,768]{1,0:T(8,128)(2,1)} async-done(((bf16[1024,768]{1,0:T(8,128)(2,1)}), bf16[4096,768]{1,0:T(8,128)(2,1)}) %all-gather.19.cloned.1.call-update) | async-done | bytes 6291472 | tf_op jit(solution)/shard_map/all_gather | solution.py:54
  675.0 6.6 fusion.87
  681.7 60.5 %reduce-scatter.19.cloned.1.call-done = f32[1024,192]{0,1:T(8,128)} async-done(((f32[4096,192]{0,1:T(8,128)}), f32[1024,192]{0,1:T(8,128)}) %reduce-scatter.19.cloned.1.call-update) | async-done | bytes 786448 | tf_op jit(solution)/shard_map/reduce_scatter | solution.py:62
  742.2 1.5 multiply_reduce_fusion.1
  743.7 8.2 all-reduce.3
  751.9 2.2 convert_reduce_fusion.5
  754.2 37.0 %all-gather.21.cloned.1.call-done = bf16[4096,192]{0,1:T(8,128)(2,1)} async-done(((bf16[1024,192]{0,1:T(8,128)(2,1)}), bf16[4096,192]{0,1:T(8,128)(2,1)}) %all-gather.21.cloned.1.call-update) | async-done | bytes 1572880 | tf_op jit(solution)/shard_map/all_gather | solution.py:36
  791.2 3.6 fusion.90
  795.7 42.1 %reduce-scatter.21.cloned.1.call-done = f32[1024,192]{0,1:T(8,128)} async-done(((f32[4096,192]{0,1:T(8,128)}), f32[1024,192]{0,1:T(8,128)}) %reduce-scatter.21.cloned.1.call-update) | async-done | bytes 786448 | tf_op jit(solution)/shard_map/reduce_scatter | solution.py:44
  837.9 1.2 convert_element_type.160
  841.0 10.7 while.27
  845.0 1.3 fusion.146
  846.4 1.0 subtract_exponential_fusion.3
  850.4 1.3 fusion.146
  852.4 1.4 copy.40
  854.0 1.4 copy.41
  855.7 1.2 pad_maximum_fusion
  857.0 5.4 convolution_convert_fusion.1
  862.3 47.4 %all-gather.15.cloned.1.call-done = bf16[4096,768]{1,0:T(8,128)(2,1)} async-done(((bf16[1024,768]{1,0:T(8,128)(2,1)}), bf16[4096,768]{1,0:T(8,128)(2,1)}) %all-gather.15.cloned.1.call-update) | async-done | bytes 6291472 | tf_op jit(solution)/shard_map/all_gather | solution.py:54
  909.8 5.5 fusion.54
  915.3 1.2 convolution_convert_fusion.3
  916.5 51.9 %all-gather.23.cloned.1.call-done = bf16[4096,576]{0,1:T(8,128)(2,1)} async-done(((bf16[1024,576]{0,1:T(8,128)(2,1)}), bf16[4096,576]{0,1:T(8,128)(2,1)}) %all-gather.23.cloned.1.call-update) | async-done | bytes 4718608 | tf_op jit(solution)/shard_map/all_gather | solution.py:54
  968.4 4.7 convolution_convert_fusion.2
  974.1 5.5 fusion.88
  980.5 6.8 fusion.85
  987.6 1.2 convert_reduce_fusion.3
  988.9 15.1 %all-reduce.1 = (f32[2,192]{1,0:T(2,128)}, f32[768]{0:T(1024)}) all-reduce(f32[2,192]{1,0:T(2,128)S(1)} %pad_maximum_fusion.3, f32[768]{0:T(1024)S(1)} %get-tuple-element.183), channel_id=1, replica_groups=mesh['dp'=2,'row'=4,'col'=4] {'dp','row'}, use_global_device_ids=true, to_apply=%region_42.43 | all-reduce | flops 1152 | bytes 9216 | tf_op jit(solution)/shard_map/psum | solution.py:220
  1004.0 1.8 convert_element_type.177
  1005.8 1.8 convert_element_type.181
  1007.6 1.9 copy.43
  1009.6 1.6 convert_element_type.175
  1011.2 46.3 %reduce-scatter.23.cloned.1.call-done = f32[1024,192]{0,1:T(8,128)} async-done(((f32[4096,192]{0,1:T(8,128)}), f32[1024,192]{0,1:T(8,128)}) %reduce-scatter.23.cloned.1.call-update) | async-done | bytes 786448 | tf_op jit(solution)/shard_map/reduce_scatter | solution.py:62
  1057.5 1.5 fusion.70
  1059.0 8.2 all-reduce.2
  1067.2 52.8 %reduce-scatter.15.cloned.1.call-done = f32[1024,192]{0,1:T(8,128)} async-done(((f32[4096,192]{0,1:T(8,128)}), f32[1024,192]{0,1:T(8,128)}) %reduce-scatter.15.cloned.1.call-update) | async-done | bytes 786448 | tf_op jit(solution)/shard_map/reduce_scatter | solution.py:62
  1120.0 2.8 fusion.74
  1122.8 16.6 %all-reduce = (f32[2,192]{1,0:T(2,128)}, f32[4,192]{1,0:T(4,128)}) all-reduce(f32[2,192]{1,0:T(2,128)S(1)} %pad_maximum_fusion.2, f32[4,192]{1,0:T(4,128)S(1)} %pad_maximum_fusion.1), channel_id=1, replica_groups=mesh['dp'=2,'row'=4,'col'=4] {'dp','col'}, use_global_device_ids=true, to_apply=%region_33.34 | all-reduce | flops 1152 | bytes 9216 | tf_op jit(solution)/shard_map/psum | solution.py:219
  (136 shorter events, 25.1 us)
Async XLA Ops:
  7.2 345.1 %copy-start = (bf16[192,768]{1,0:T(8,128)(2,1)S(1)}, bf16[192,768]{1,0:T(8,128)(2,1)}, u32[]{:S(2)}) copy-start(bf16[192,768]{1,0:T(8,128)(2,1)} %param.20) | copy-start | bytes 884740
  7.2 61.2 %all-gather.9.cloned.1.call-start = ((), (), s32[]{:S(2)}) async-start(), calls=%async_computation.8 | async-start | bytes 1966080 | tf_op jit(solution)/shard_map/all_gather | solution.py:36
  30.9 137.9 %reduce-scatter.9.cloned.1.call-start = ((), (), s32[]{:S(2)}) async-start(), calls=%async_computation.9 | async-start | bytes 11796480 | tf_op jit(solution)/shard_map/reduce_scatter | solution.py:44
  32.1 42.7 %copy-start.7 = (bf16[192,3,192]{0,2,1:T(8,128)(2,1)}, bf16[192,3,192]{0,2,1:T(8,128)(2,1)S(1)}, u32[]{:S(2)}) copy-start(bf16[192,3,192]{0,2,1:T(8,128)(2,1)S(1)} %copy.30) | copy-start | bytes 663556
  74.8 0.7 copy-start.16
  74.9 136.8 %all-gather.11.cloned.1.call-start = ((), (), s32[]{:S(2)}) async-start(), calls=%async_computation.10 | async-start | bytes 1966080 | tf_op jit(solution)/shard_map/all_gather | solution.py:54
  174.0 37.7 %copy-start.14 = (bf16[192,192]{1,0:T(8,128)(2,1)S(1)}, bf16[192,192]{1,0:T(8,128)(2,1)}, u32[]{:S(2)}) copy-start(bf16[192,192]{1,0:T(8,128)(2,1)} %param.19) | copy-start | bytes 221188
  180.7 95.3 %reduce-scatter.11.cloned.1.call-start = ((), (), s32[]{:S(2)}) async-start(), calls=%async_computation.11 | async-start | bytes 3932160 | tf_op jit(solution)/shard_map/reduce_scatter | solution.py:62
  215.4 60.6 %copy-start.2 = (bf16[192,1024]{1,0:T(8,128)(2,1)S(1)}, bf16[192,1024]{1,0:T(8,128)(2,1)}, u32[]{:S(2)}) copy-start(bf16[192,1024]{1,0:T(8,128)(2,1)} %param.14) | copy-start | bytes 1179652
  215.4 98.9 %copy-start.12 = (bf16[192,768]{1,0:T(8,128)(2,1)S(1)}, bf16[192,768]{1,0:T(8,128)(2,1)}, u32[]{:S(2)}) copy-start(bf16[192,768]{1,0:T(8,128)(2,1)} %param.22) | copy-start | bytes 884740
  215.4 98.9 %all-gather.17.cloned.1.call-start = ((), (), s32[]{:S(2)}) async-start(), calls=%async_computation.16 | async-start | bytes 1966080 | tf_op jit(solution)/shard_map/all_gather | solution.py:36
  216.0 136.2 %all-gather.13.cloned.1.call-start = ((), (), s32[]{:S(2)}) async-start(), calls=%async_computation.12 | async-start | bytes 1966080 | tf_op jit(solution)/shard_map/all_gather | solution.py:36
  296.1 178.7 %reduce-scatter.17.cloned.1.call-start = ((), (), s32[]{:S(2)}) async-start(), calls=%async_computation.17 | async-start | bytes 15728640 | tf_op jit(solution)/shard_map/reduce_scatter | solution.py:44
  322.2 276.4 %reduce-scatter.13.cloned.1.call-start = ((), (), s32[]{:S(2)}) async-start(), calls=%async_computation.13 | async-start | bytes 15728640 | tf_op jit(solution)/shard_map/reduce_scatter | solution.py:44
  360.0 238.6 %copy-start.15 = (f32[768]{0:T(1024)S(1)}, f32[768]{0:T(1024)}, u32[]{:S(2)}) copy-start(f32[768]{0:T(1024)} %param.21) | copy-start | bytes 9220
  360.0 315.0 %all-gather.19.cloned.1.call-start = ((), (), s32[]{:S(2)}) async-start(), calls=%async_computation.18 | async-start | bytes 7864320 | tf_op jit(solution)/shard_map/all_gather | solution.py:54
  604.8 137.4 %reduce-scatter.19.cloned.1.call-start = ((), (), s32[]{:S(2)}) async-start(), calls=%async_computation.19 | async-start | bytes 3932160 | tf_op jit(solution)/shard_map/reduce_scatter | solution.py:62
  681.6 70.3 %copy-start.5 = (bf16[192,1024]{1,0:T(8,128)(2,1)S(1)}, bf16[192,1024]{1,0:T(8,128)(2,1)}, u32[]{:S(2)}) copy-start(bf16[192,1024]{1,0:T(8,128)(2,1)} %param.23) | copy-start | bytes 1179652
  681.7 109.6 %all-gather.21.cloned.1.call-start = ((), (), s32[]{:S(2)}) async-start(), calls=%async_computation.20 | async-start | bytes 1966080 | tf_op jit(solution)/shard_map/all_gather | solution.py:36
  754.2 83.7 %reduce-scatter.21.cloned.1.call-start = ((), (), s32[]{:S(2)}) async-start(), calls=%async_computation.21 | async-start | bytes 3932160 | tf_op jit(solution)/shard_map/reduce_scatter | solution.py:44
  794.9 114.8 %all-gather.15.cloned.1.call-start = ((), (), s32[]{:S(2)}) async-start(), calls=%async_computation.14 | async-start | bytes 7864320 | tf_op jit(solution)/shard_map/all_gather | solution.py:54
  795.7 172.8 %all-gather.23.cloned.1.call-start = ((), (), s32[]{:S(2)}) async-start(), calls=%async_computation.22 | async-start | bytes 5898240 | tf_op jit(solution)/shard_map/all_gather | solution.py:54
  842.7 1.0 copy-start.9
  844.3 0.8 copy-start.10
  848.0 1.1 copy-start.9
  849.6 0.8 copy-start.10
  856.9 147.1 %all-reduce.7.cloned.1.call-start = ((), (), s32[]{:S(2)}) async-start(), calls=%async_computation.24 | async-start | bytes 1966080 | tf_op jit(solution)/shard_map/psum | solution.py:212
  909.8 5.5 copy-start.4
  909.8 5.5 copy-start.11
  916.5 57.6 %copy-start.8 = (bf16[192,3,192]{0,2,1:T(8,128)(2,1)S(1)}, bf16[192,3,192]{0,2,1:T(8,128)(2,1)}, u32[]{:S(2)}) copy-start(bf16[192,3,192]{0,2,1:T(8,128)(2,1)} %copy-done.7) | copy-start | bytes 663556
  974.0 83.5 %reduce-scatter.23.cloned.1.call-start = ((), (), s32[]{:S(2)}) async-start(), calls=%async_computation.23 | async-start | bytes 3932160 | tf_op jit(solution)/shard_map/reduce_scatter | solution.py:62
  979.6 1.0 copy-start.13
  979.6 140.4 %reduce-scatter.15.cloned.1.call-start = ((), (), s32[]{:S(2)}) async-start(), calls=%async_computation.15 | async-start | bytes 3932160 | tf_op jit(solution)/shard_map/reduce_scatter | solution.py:62
  987.3 132.7 %copy-start.3 = (f32[1024,192]{0,1:T(8,128)S(1)}, f32[1024,192]{0,1:T(8,128)}, u32[]{:S(2)}) copy-start(f32[1024,192]{0,1:T(8,128)} %reduce-scatter.19.cloned.1.call-done) | copy-start | bytes 2359300
  987.3 132.7 %copy-start.6 = (bf16[192,1024]{1,0:T(8,128)(2,1)S(1)}, bf16[192,1024]{1,0:T(8,128)(2,1)}, u32[]{:S(2)}) copy-start(bf16[192,1024]{1,0:T(8,128)(2,1)} %param.23) | copy-start | bytes 1179652
  1009.6 129.9 %copy-start.1 = (bf16[192,768]{1,0:T(8,128)(2,1)S(1)}, bf16[192,768]{1,0:T(8,128)(2,1)}, u32[]{:S(2)}) copy-start(bf16[192,768]{1,0:T(8,128)(2,1)} %param.20) | copy-start | bytes 884740
Sparse Core Ops, SparseCore 0:
  31.0 37.3 all-gather.8
  75.0 93.7 reduce-scatter.8
  180.8 30.8 all-gather.10
  215.5 60.3 reduce-scatter.10
  277.4 36.9 all-gather.16
  316.3 35.8 all-gather.12
  355.3 119.4 reduce-scatter.16
  477.9 120.5 reduce-scatter.12
  604.9 70.0 all-gather.18
  681.8 60.3 reduce-scatter.18
  754.3 36.8 all-gather.20
  795.0 42.7 reduce-scatter.20
  839.7 70.0 all-gather.14
  911.5 56.9 all-gather.22
  974.1 19.8 all-reduce.6
  996.2 61.3 reduce-scatter.22
  1059.7 60.3 reduce-scatter.14
where the time goes:
time: 1150 us
  waiting for transfers between devices  916 us (80%)
  blocking collectives  83.8 us (7%)
  matrix products  76.4 us (7%)
  other arithmetic  34 us (3%)
  local copies, waits for them, and re-layouts  19.9 us (2%)
  between operations  14.3 us (1%)
    reduce_scatter x4, waiting for transfers between devices, across_cols(): lax.psum_scatter(partial_rows(jnp.int32(0), lax.axis_size('row') * share)...  374 us
    reduce_scatter x4, waiting for transfers between devices, across_rows(): lax.psum_scatter(partial_rows(jnp.int32(0), lax.axis_size('col') * share)...  219 us
    all_gather x4, waiting for transfers between devices, across_rows(): gathered = lax.all_gather(local, 'row', axis=0, tiled=True)  200 us
    all_gather x4, waiting for transfers between devices, across_cols(): gathered = lax.all_gather(local, 'col', axis=0, tiled=True)  121 us
    dot_general x4, matrix products, multiply(): return jnp.dot(rows, weight, preferred_element_type=jnp.float32)  25.7 us
  transfers between devices with their start and end apart: 17, of which 16 were waited for; matrix products, arithmetic and copies ran while one was open for 6% of the time, Pallas kernels for 0%

commit v1 on v0

v1 whole, which is shorter than its diff:
```python
import jax
import jax.numpy as jnp
from jax import lax
from jax.sharding import PartitionSpec as P

D = 768
HEAD = 64
LENGTH = 512


EPSILON = 1e-05
GELU_COEF = 0.7978845608028654


def gelu_tanh(values):
    return (
        0.5 * values * (1.0 + jnp.tanh(GELU_COEF * (values + 0.044715 * values * values * values)))
    )


def multiply(rows, weight, flipped):
    if flipped:
        return lax.dot_general(
            rows, weight, (((1,), (1,)), ((), ())), preferred_element_type=jnp.float32
        )
    return jnp.dot(rows, weight, preferred_element_type=jnp.float32)


def contract_tokens(left, right):
    return lax.dot_general(
        left, right, (((0,), (0,)), ((), ())), preferred_element_type=jnp.float32
    )


def gather(local, axis_name):
    return lax.all_gather(local, axis_name, axis=0, tiled=True)


def scatter_sum(partial, axis_name):
    return lax.psum_scatter(
        partial.astype(jnp.bfloat16), axis_name, scatter_dimension=0, tiled=True
    ).astype(jnp.float32)


def to_tokens(block):
    rows, cols = lax.axis_size("row"), lax.axis_size("col")
    block = lax.all_to_all(block, "row", split_axis=1, concat_axis=0, tiled=True)
    moves = [(r * cols + c, c * rows + r) for r in range(rows) for c in range(cols)]
    return lax.ppermute(block, ("row", "col"), moves).T


def to_features(tokens):
    rows, cols = lax.axis_size("row"), lax.axis_size("col")
    moves = [(c * rows + r, r * cols + c) for r in range(rows) for c in range(cols)]
    block = lax.ppermute(tokens.T, ("row", "col"), moves)
    return lax.all_to_all(block, "row", split_axis=0, concat_axis=1, tiled=True)


def norm_forward(values, gain, bias):
    center = jnp.mean(values, axis=1, keepdims=True)
    offset = values - center
    inverse = lax.rsqrt(jnp.mean(offset * offset, axis=1, keepdims=True) + EPSILON)
    normal = offset * inverse
    return (normal * gain + bias, normal, inverse)


def norm_backward(grad, gain, normal, inverse):
    scaled = grad * gain
    first = jnp.mean(scaled, axis=1, keepdims=True)
    second = jnp.mean(scaled * normal, axis=1, keepdims=True)
    result = inverse * (scaled - first - normal * second)
    return (result, jnp.sum(grad * normal, axis=0), jnp.sum(grad, axis=0))


def causal_mask(length):
    positions = jnp.arange(length)
    return positions[None, :] <= positions[:, None]


def attention_forward(queries, keys, values):
    factor = HEAD ** (-0.5)

    def one_sequence(pieces):
        seq_q, seq_k, seq_v = pieces
        scores = (
            jnp.einsum("qhd,khd->hqk", seq_q, seq_k, preferred_element_type=jnp.float32) * factor
        )
        scores = jnp.where(causal_mask(seq_q.shape[0])[None], scores, -1e30)
        summit = jnp.max(scores, axis=-1, keepdims=True)
        expos = jnp.exp(scores - summit)
        total = jnp.sum(expos, axis=-1, keepdims=True)
        probs = (expos / total).astype(jnp.bfloat16)
        output = jnp.einsum("hqk,khd->qhd", probs, seq_v, preferred_element_type=jnp.float32)
        return (output, summit[..., 0] + jnp.log(total[..., 0]))

    return lax.map(one_sequence, (queries, keys, values))


def attention_backward(queries, keys, values, grad_out, log_sums):
    factor = HEAD ** (-0.5)

    def one_sequence(pieces):
        seq_q, seq_k, seq_v, seq_g, seq_l = pieces
        scores = (
            jnp.einsum("qhd,khd->hqk", seq_q, seq_k, preferred_element_type=jnp.float32) * factor
        )
        scores = jnp.where(causal_mask(seq_q.shape[0])[None], scores, -1e30)
        probs = jnp.exp(scores - seq_l[..., None])
        grad_v = jnp.einsum(
            "hqk,qhd->khd", probs.astype(jnp.bfloat16), seq_g, preferred_element_type=jnp.float32
        )
        grad_p = jnp.einsum("qhd,khd->hqk", seq_g, seq_v, preferred_element_type=jnp.float32)
        inner = jnp.sum(grad_p * probs, axis=-1, keepdims=True)
        grad_s = (probs * (grad_p - inner)).astype(jnp.bfloat16)
        grad_q = (
            jnp.einsum("hqk,khd->qhd", grad_s, seq_k, preferred_element_type=jnp.float32) * factor
        )
        grad_k = (
            jnp.einsum("hqk,qhd->khd", grad_s, seq_q, preferred_element_type=jnp.float32) * factor
        )
        return (grad_q, grad_k, grad_v)

    return lax.map(one_sequence, (queries, keys, values, grad_out, log_sums))


def body(
    block_input, norm_gains, row_biases, w_qkv, qv_bias, w_out, w_up, up_bias, w_down, cotangent
):
    head_cols = w_qkv.shape[2]
    inputs = to_tokens(block_input).astype(jnp.float32)
    cot = to_tokens(cotangent)
    vectors = gather(jnp.concatenate([norm_gains, row_biases], axis=0).T, "row").T
    gains, biases = vectors[:2], vectors[2:]
    qkv_weight = gather(w_qkv.reshape(w_qkv.shape[0], -1), "row")
    rest = gather(jnp.concatenate([w_out.T, w_up, w_down], axis=1), "row")
    width = w_up.shape[1]
    out_t = rest[:, :head_cols]
    up = rest[:, head_cols : head_cols + width]
    down = rest[:, head_cols + width :]

    normed_one, normal_one, inverse_one = norm_forward(inputs, gains[0], biases[0])
    source_one = gather(normed_one.astype(jnp.bfloat16), "col")
    qkv_sum = multiply(source_one, qkv_weight, False)
    rows_here = qkv_sum.shape[0]
    qkv_sum = qkv_sum.reshape(rows_here, 3, head_cols)
    shape_four = (rows_here // LENGTH, LENGTH, head_cols // HEAD, HEAD)
    queries = (qkv_sum[:, 0] + qv_bias[0]).astype(jnp.bfloat16).reshape(shape_four)
    keys_all = qkv_sum[:, 1].astype(jnp.bfloat16).reshape(shape_four)
    values_all = (qkv_sum[:, 2] + qv_bias[1]).astype(jnp.bfloat16).reshape(shape_four)
    attended, log_sums = attention_forward(queries, keys_all, values_all)
    attended_low = attended.reshape(rows_here, head_cols).astype(jnp.bfloat16)
    middle = inputs + scatter_sum(multiply(attended_low, out_t, True), "col") + biases[2]
    normed_two, normal_two, inverse_two = norm_forward(middle, gains[1], biases[1])
    source_two = gather(normed_two.astype(jnp.bfloat16), "col")
    cot_all = gather(cot, "col")
    before = multiply(source_two, up, False) + up_bias
    hidden_low = gelu_tanh(before).astype(jnp.bfloat16)
    grad_hidden = multiply(cot_all, down, False)
    grad_before = jax.vjp(gelu_tanh, before)[1](grad_hidden)[0].astype(jnp.bfloat16)
    grad_normed_two = scatter_sum(multiply(grad_before, up, True), "col")
    output = middle + scatter_sum(multiply(hidden_low, down, True), "col") + biases[3]
    grad_w_down = contract_tokens(cot_all, hidden_low)
    grad_up_bias = jnp.sum(grad_before.astype(jnp.float32), axis=0)
    grad_w_up = contract_tokens(source_two, grad_before)
    grad_out = cot.astype(jnp.float32)
    back_two, gain_two, shift_two = norm_backward(
        grad_normed_two, gains[1], normal_two, inverse_two
    )
    grad_middle = grad_out + back_two
    grad_middle_low = grad_middle.astype(jnp.bfloat16)
    grad_out_bias = jnp.sum(grad_middle_low.astype(jnp.float32), axis=0)
    grad_down_bias = jnp.sum(grad_out, axis=0)
    grad_middle_all = gather(grad_middle_low, "col")
    grad_att_low = multiply(grad_middle_all, out_t, False).astype(jnp.bfloat16).reshape(shape_four)
    grad_w_out_t = contract_tokens(grad_middle_all, attended_low)
    grad_q, grad_k, grad_v = attention_backward(
        queries, keys_all, values_all, grad_att_low, log_sums
    )
    grad_q = grad_q.reshape(rows_here, head_cols).astype(jnp.bfloat16)
    grad_k = grad_k.reshape(rows_here, head_cols).astype(jnp.bfloat16)
    grad_v = grad_v.reshape(rows_here, head_cols).astype(jnp.bfloat16)
    grad_qkv_low = jnp.concatenate([grad_q, grad_k, grad_v], axis=1)
    grad_qv = jnp.stack(
        [jnp.sum(grad_q.astype(jnp.float32), axis=0), jnp.sum(grad_v.astype(jnp.float32), axis=0)]
    )
    grad_normed_one = scatter_sum(multiply(grad_qkv_low, qkv_weight, True), "col")
    grad_w_qkv = contract_tokens(source_one, grad_qkv_low)
    back_one, gain_one, shift_one = norm_backward(
        grad_normed_one, gains[0], normal_one, inverse_one
    )
    grad_input = grad_middle + back_one

    mlp_sum = scatter_sum(
        jnp.concatenate([grad_w_out_t, grad_w_up, grad_w_down], axis=1), "row"
    )
    qkv_grad = scatter_sum(grad_w_qkv, "row")
    weights_sum = lax.psum(
        jnp.concatenate([mlp_sum, qkv_grad], axis=1).astype(jnp.bfloat16), "dp"
    ).astype(jnp.float32)
    sum_out = weights_sum[:, :head_cols].T
    sum_up = weights_sum[:, head_cols : head_cols + width]
    sum_down = weights_sum[:, head_cols + width : head_cols + 2 * width]
    sum_qkv = weights_sum[:, head_cols + 2 * width :].reshape(w_qkv.shape)
    small = jnp.stack([gain_one, gain_two, shift_one, shift_two, grad_out_bias, grad_down_bias])
    small = lax.psum(small, ("dp", "row", "col"))
    share = norm_gains.shape[1]
    small = lax.dynamic_slice_in_dim(small, lax.axis_index("row") * share, share, axis=1)
    sum_qv, sum_upb = lax.psum((grad_qv, grad_up_bias), ("dp", "row"))
    return (
        to_features(output.astype(jnp.bfloat16)),
        to_features(grad_input.astype(jnp.bfloat16)),
        small[:2],
        small[2:],
        sum_qkv,
        sum_qv,
        sum_out,
        sum_up,
        sum_upb,
        sum_down,
    )


def solution(mesh):
    in_specs = (
        P("row", ("dp", "col")),
        P(None, "row"),
        P(None, "row"),
        P("row", None, "col"),
        P(None, "col"),
        P("col", "row"),
        P("row", "col"),
        P("col"),
        P("row", "col"),
        P("row", ("dp", "col")),
    )
    out_specs = (
        P("row", ("dp", "col")),
        P("row", ("dp", "col")),
        P(None, "row"),
        P(None, "row"),
        P("row", None, "col"),
        P(None, "col"),
        P("col", "row"),
        P("row", "col"),
        P("col"),
        P("row", "col"),
    )
    return jax.shard_map(body, mesh=mesh, in_specs=in_specs, out_specs=out_specs, check_vma=False)
```

time: 1150 us -> 650 us (0.57)
  waiting for transfers between devices: 916 us -> 402 us
  matrix products: 76.4 us -> 51.3 us
  starting transfers between devices: 1.1 us -> 20.1 us
  blocking collectives: 83.8 us -> 99.9 us
  other arithmetic: 34 us -> 19.6 us
  local copies, waits for them, and re-layouts: 19.9 us -> 32.2 us
    reduce_scatter x8 -> x4, waiting for transfers between devices: 593 us -> 125 us  [scatter_sum(): lax.psum_scatter(partial.astype(jnp.bfloat16), axis_name, scatter_dimensi...]
    all_gather x8 -> x5, waiting for transfers between devices: 322 us -> 124 us  [gather(): return lax.all_gather(local, axis_name, axis=0, tiled=True)]
    ppermute x0 -> x4, waiting for transfers between devices: none -> 111 us  [the longest x2 58.2 us: to_tokens(): return lax.ppermute(block, ('row', 'col'), moves).T]
    unnamed x17 -> x14, waiting for transfers between devices: 1.48 us -> 41.3 us
    psum x7 -> x1, blocking collectives: 68.7 us -> 40.5 us  [body(): small = lax.psum(small, ('dp', 'row', 'col'))]
    all_gather x0 -> x2, blocking collectives: none -> 24.7 us  [gather(): return lax.all_gather(local, axis_name, axis=0, tiled=True)]
    all_to_all x0 -> x2, blocking collectives: none -> 19.7 us  [to_tokens(): lax.all_to_all(block, 'row', split_axis=1, concat_axis=0, tiled=True)]
    ppermute x0 -> x4, starting transfers between devices: none -> 12.1 us  [the longest x2 6.33 us: to_tokens(): return lax.ppermute(block, ('row', 'col'), moves).T]
  transfers between devices with their start and end apart: 17 -> 18, of which waited for: 16 -> 13; matrix products, arithmetic and copies ran while one was open for 6% -> 8% of each run, Pallas kernels for 0% -> 0%
where the time goes in v1:
time: 650 us; the launch traced here: 641 us
  waiting for transfers between devices  402 us (62%)
  blocking collectives  99.9 us (15%)
  matrix products  51.3 us (8%)
  local copies, waits for them, and re-layouts  32.2 us (5%)
  starting transfers between devices  20.1 us (3%)
  other arithmetic  19.6 us (3%)
  between operations  15.4 us (2%)
    reduce_scatter x4, waiting for transfers between devices, scatter_sum(): lax.psum_scatter(partial.astype(jnp.bfloat16), axis_name, scatter_dimensi...  125 us
    all_gather x5, waiting for transfers between devices, gather(): return lax.all_gather(local, axis_name, axis=0, tiled=True)  124 us
    ppermute x2, waiting for transfers between devices, to_tokens(): return lax.ppermute(block, ('row', 'col'), moves).T  58.2 us
    ppermute x2, waiting for transfers between devices, to_features(): block = lax.ppermute(tokens.T, ('row', 'col'), moves)  53 us
    unnamed x14, waiting for transfers between devices  41.3 us
    psum x1, blocking collectives, body(): small = lax.psum(small, ('dp', 'row', 'col'))  40.5 us
    all_gather x2, blocking collectives, gather(): return lax.all_gather(local, axis_name, axis=0, tiled=True)  24.7 us
    all_to_all x2, blocking collectives, to_tokens(): lax.all_to_all(block, 'row', split_axis=1, concat_axis=0, tiled=True)  19.7 us
  transfers between devices with their start and end apart: 18, of which 13 were waited for; matrix products, arithmetic and copies ran while one was open for 8% of the time, Pallas kernels for 0%

profile of v1, /device:TPU:2, one launch (start us, length us, event | category | flops | bytes accessed | tf_op | source)
XLA Modules:
  0.0 640.6 jit_solution(3045952631467766267)
XLA Ops:
  7.3 1.1 copy.145
  8.3 10.1 %all_to_all.76 = bf16[192,4,256]{2,0,1:T(8,128)(2,1)S(1)} all-to-all(bf16[192,4,256]{2,0,1:T(8,128)(2,1)S(1)} %bitcast.275), channel_id=1, replica_groups=mesh['dp'=2,'row'=4,'col'=4] {'row'}, dimensions={1} | all-to-all | bytes 786432 | tf_op jit(solution)/shard_map/all_to_all | solution.py:47
  18.6 4.0 collective-permute-start
  23.3 13.2 %all-gather = f32[4,192,6]{1,2,0:T(8,128)S(1)} all-gather(f32[1,192,6]{1,2,0:T(8,128)S(1)} %maximum_bitcast_fusion), channel_id=1, replica_groups=mesh['dp'=2,'row'=4,'col'=4] {'row'}, dimensions={0}, use_global_device_ids=true | all-gather | bytes 23040 | tf_op jit(solution)/shard_map/all_gather | solution.py:36
  36.7 11.3 %collective-permute-done = bf16[768,256]{0,1:T(8,128)(2,1)S(1)} collective-permute-done((bf16[768,256]{0,1:T(8,128)(2,1)S(1)}, bf16[768,256]{0,1:T(8,128)(2,1)S(1)}, u32[]{:S(2)}, u32[]{:S(2)}) %collective-permute-start) | collective-permute-done | bytes 393248 | tf_op jit(solution)/shard_map/ppermute | solution.py:49
  48.4 1.0 fusion.76
  49.6 1.3 concatenate.18
  51.6 11.5 %all_gather.23 = bf16[768,576]{1,0:T(8,128)(2,1)S(1)} all-gather(bf16[192,576]{1,0:T(8,128)(2,1)S(1)} %copy.101), channel_id=1, replica_groups=mesh['dp'=2,'row'=4,'col'=4] {'row'}, dimensions={0}, use_global_device_ids=true | all-gather | bytes 1105920 | tf_op jit(solution)/shard_map/all_gather | solution.py:36
  63.0 23.8 %all-gather.7.cloned.1.call-done = bf16[1024,768]{1,0:T(8,128)(2,1)} async-done(((bf16[256,768]{1,0:T(8,128)(2,1)}), bf16[1024,768]{1,0:T(8,128)(2,1)}) %all-gather.7.cloned.1.call-update) | async-done | bytes 1572880 | tf_op jit(solution)/shard_map/all_gather | solution.py:36
  86.9 2.5 fusion.96
  92.1 5.4 while.26
  93.7 1.1 fusion.133
  96.4 1.1 fusion.133
  97.9 30.2 %all-gather.9.cloned.1.call-done = bf16[768,1728]{1,0:T(8,128)(2,1)} async-done(((bf16[192,1728]{1,0:T(8,128)(2,1)}), bf16[768,1728]{1,0:T(8,128)(2,1)}) %all-gather.9.cloned.1.call-update) | async-done | bytes 2654224 | tf_op jit(solution)/shard_map/all_gather | solution.py:36
  128.2 2.8 convolution_convert_fusion.3
  131.0 35.5 %reduce-scatter.11.cloned.1.call-done = bf16[256,768]{1,0:T(8,128)(2,1)} async-done(((bf16[1024,768]{1,0:T(8,128)(2,1)}), bf16[256,768]{1,0:T(8,128)(2,1)}) %reduce-scatter.11.cloned.1.call-update) | async-done | bytes 393232 | tf_op jit(solution)/shard_map/reduce_scatter | solution.py:40
  166.6 1.2 fusion.93
  167.8 1.3 multiply_reduce_fusion.1
  169.1 2.0 add_convert_fusion.1
  171.2 9.6 %all_to_all.77 = bf16[192,4,256]{2,0,1:T(8,128)(2,1)S(1)} all-to-all(bf16[192,4,256]{2,0,1:T(8,128)(2,1)S(1)} %bitcast.276), channel_id=1, replica_groups=mesh['dp'=2,'row'=4,'col'=4] {'row'}, dimensions={1} | all-to-all | bytes 786432 | tf_op jit(solution)/shard_map/all_to_all | solution.py:47
  181.0 2.3 collective-permute-start.2
  183.3 46.9 %collective-permute-done.2 = bf16[768,256]{0,1:T(8,128)(2,1)S(1)} collective-permute-done((bf16[768,256]{0,1:T(8,128)(2,1)S(1)}, bf16[768,256]{0,1:T(8,128)(2,1)S(1)}, u32[]{:S(2)}, u32[]{:S(2)}) %collective-permute-start.2) | collective-permute-done | bytes 393248 | tf_op jit(solution)/shard_map/ppermute | solution.py:49
  231.2 5.0 fusion.67
  236.1 34.2 %all-gather.13.cloned.1.call-done = bf16[1024,768]{1,0:T(8,128)(2,1)} async-done(((bf16[256,768]{1,0:T(8,128)(2,1)}), bf16[1024,768]{1,0:T(8,128)(2,1)}) %all-gather.13.cloned.1.call-update) | async-done | bytes 1572880 | tf_op jit(solution)/shard_map/all_gather | solution.py:36
  270.3 6.6 %convert_reduce_fusion = (f32[768]{0:T(1024)S(1)}, bf16[1024,768]{1,0:T(8,128)(2,1)S(1)}) fusion(bf16[1024,768]{1,0:T(8,128)(2,1)} %all-gather.13.cloned.1.call-done, bf16[768,1728]{1,0:T(8,128)(2,1)} %all-gather.9.cloned.1.call-done, f32[1024,768]{1,0:T(8,128)} %fusion.67, f32[768]{0:T(1024)S(1)} %copy-done.23), kind=kOutput, calls=%fused_computation.71 | convolution fusion | flops 1229192448 | bytes 7477248 | tf_op jit(solution)/shard_map/dot_general | solution.py:26
  276.9 1.1 copy-done.25
  278.1 4.1 convolution_convert_fusion.1
  282.2 5.8 convolution_convert_fusion.2
  288.1 28.6 %reduce-scatter.15.cloned.1.call-done = bf16[256,768]{1,0:T(8,128)(2,1)} async-done(((bf16[1024,768]{1,0:T(8,128)(2,1)}), bf16[256,768]{1,0:T(8,128)(2,1)}) %reduce-scatter.15.cloned.1.call-update) | async-done | bytes 393232 | tf_op jit(solution)/shard_map/reduce_scatter | solution.py:40
  316.6 1.5 fusion.87
  318.2 35.1 %reduce-scatter.13.cloned.1.call-done = bf16[256,768]{1,0:T(8,128)(2,1)} async-done(((bf16[1024,768]{1,0:T(8,128)(2,1)}), bf16[256,768]{1,0:T(8,128)(2,1)}) %reduce-scatter.13.cloned.1.call-update) | async-done | bytes 393232 | tf_op jit(solution)/shard_map/reduce_scatter | solution.py:40
  353.2 2.8 convert_reduce_fusion.7
  356.4 35.8 %all-gather.15.cloned.1.call-done = bf16[1024,768]{1,0:T(8,128)(2,1)} async-done(((bf16[256,768]{1,0:T(8,128)(2,1)}), bf16[1024,768]{1,0:T(8,128)(2,1)}) %all-gather.15.cloned.1.call-update) | async-done | bytes 1572880 | tf_op jit(solution)/shard_map/all_gather | solution.py:36
  392.1 2.1 convolution_convert_fusion.7
  395.4 9.3 %while.27 = (s32[]{:T(128)}, bf16[2,512,3,64]{1,3,2,0:T(8,128)(2,1)S(1)}, bf16[2,512,3,64]{1,3,2,0:T(8,128)(2,1)}, bf16[2,512,3,64]{1,3,2,0:T(8,128)(2,1)S(1)}, ...) while((s32[]{:T(128)}, ...), condition=%wide.region_15.16_spmd, body=%wide.region_13.15_spmd.sunk | while | flops 510851584 | bytes 29856936 | solution.py:123
  395.6 1.0 subtract_exponential_fusion.3
  400.2 1.0 subtract_exponential_fusion.3
  404.8 1.5 copy.117
  407.4 1.0 copy-done.18
  408.5 2.4 convolution_convert_fusion.6
  411.0 3.9 convolution_convert_fusion
  415.2 3.6 convolution_convert_fusion.5
  418.8 2.0 fusion.57
  421.5 4.3 copy.130
  425.8 1.0 copy-done.13
  426.8 2.4 collective-permute-start.1
  429.1 27.1 %collective-permute-done.1 = bf16[768,256]{0,1:T(8,128)(2,1)S(1)} collective-permute-done((bf16[768,256]{0,1:T(8,128)(2,1)S(1)}, bf16[768,256]{0,1:T(8,128)(2,1)S(1)}, u32[]{:S(2)}, u32[]{:S(2)}) %collective-permute-start.1) | collective-permute-done | bytes 393248 | tf_op jit(solution)/shard_map/ppermute | solution.py:55
  456.2 0.9 copy.107
  457.2 3.5 all-to-all-start.1
  460.7 1.8 copy.133
  462.5 26.2 %reduce-scatter.17.cloned.1.call-done = bf16[256,768]{1,0:T(8,128)(2,1)} async-done(((bf16[1024,768]{1,0:T(8,128)(2,1)}), bf16[256,768]{1,0:T(8,128)(2,1)}) %reduce-scatter.17.cloned.1.call-update) | async-done | bytes 393232 | tf_op jit(solution)/shard_map/reduce_scatter | solution.py:40
  488.7 1.4 fusion.88
  490.2 41.1 %reduce-scatter.19.cloned.1.call-done = bf16[192,1728]{1,0:T(8,128)(2,1)} async-done(((bf16[768,1728]{1,0:T(8,128)(2,1)}), bf16[192,1728]{1,0:T(8,128)(2,1)}) %reduce-scatter.19.cloned.1.call-update) | async-done | bytes 663568
  531.3 1.4 copy.131
  532.7 2.2 pad_maximum_fusion.1
  535.3 3.4 collective-permute-start.3
  539.7 25.9 %collective-permute-done.3 = bf16[768,256]{0,1:T(8,128)(2,1)S(1)} collective-permute-done((bf16[768,256]{0,1:T(8,128)(2,1)S(1)}, bf16[768,256]{0,1:T(8,128)(2,1)S(1)}, u32[]{:S(2)}, u32[]{:S(2)}) %collective-permute-start.3) | collective-permute-done | bytes 393248 | tf_op jit(solution)/shard_map/ppermute | solution.py:55
  566.5 3.4 all-to-all-start.3
  570.3 15.0 %all-reduce = (f32[2,192]{1,0:T(2,128)}, f32[768]{0:T(1024)}) all-reduce(f32[2,192]{1,0:T(2,128)S(1)} %pad_maximum_fusion.2, f32[768]{0:T(1024)S(1)} %get-tuple-element.252), channel_id=1, replica_groups=mesh['dp'=2,'row'=4,'col'=4] {'dp','row'}, use_global_device_ids=true, to_apply=%region_31.32 | all-reduce | flops 1152 | bytes 9216 | tf_op jit(solution)/shard_map/psum | solution.py:208
  585.4 40.5 %psum.28 = f32[6,768]{1,0:T(8,128)S(1)} all-reduce(f32[6,768]{1,0:T(8,128)S(1)} %stack.36), channel_id=1, replica_groups=mesh['dp'=2,'row'=4,'col'=4] {'dp','row','col'}, use_global_device_ids=true, to_apply=%region_25.26 | all-reduce | flops 4608 | bytes 36864 | tf_op jit(solution)/shard_map/psum | solution.py:205
  628.0 1.1 slice.103
  629.1 1.1 copy.122
  630.3 1.1 copy.124
  631.4 1.1 copy.123
  (176 shorter events, 26.5 us)
Async XLA Ops:
  7.2 42.3 %copy-start.19 = (bf16[192,192]{1,0:T(8,128)(2,1)S(1)}, bf16[192,192]{1,0:T(8,128)(2,1)}, u32[]{:S(2)}) copy-start(bf16[192,192]{1,0:T(8,128)(2,1)} %param.19) | copy-start | bytes 221188
  7.2 42.4 %copy-start.17 = (bf16[192,768]{1,0:T(8,128)(2,1)S(1)}, bf16[192,768]{1,0:T(8,128)(2,1)}, u32[]{:S(2)}) copy-start(bf16[192,768]{1,0:T(8,128)(2,1)} %param.22) | copy-start | bytes 884740
  7.2 42.4 %copy-start.16 = (bf16[192,768]{1,0:T(8,128)(2,1)S(1)}, bf16[192,768]{1,0:T(8,128)(2,1)}, u32[]{:S(2)}) copy-start(bf16[192,768]{1,0:T(8,128)(2,1)} %param.20) | copy-start | bytes 884740
  7.2 79.7 %all-gather.7.cloned.1.call-start = ((), (), s32[]{:S(2)}) async-start(), calls=%async_computation.10 | async-start | bytes 1966080 | tf_op jit(solution)/shard_map/all_gather | solution.py:36
  18.4 32.6 %copy-start.20 = (f32[2,192]{1,0:T(2,128)S(1)}, f32[2,192]{1,0:T(2,128)}, u32[]{:S(2)}) copy-start(f32[2,192]{1,0:T(2,128)} %param.18) | copy-start | bytes 4612
  18.4 32.8 %copy-start.15 = (bf16[192,3,192]{2,0,1:T(8,128)(2,1)S(1)}, bf16[192,3,192]{2,0,1:T(8,128)(2,1)}, u32[]{:S(2)}) copy-start(bf16[192,3,192]{2,0,1:T(8,128)(2,1)} %param.17) | copy-start | bytes 663556
  18.6 29.4 %collective-permute-start = (bf16[768,256]{0,1:T(8,128)(2,1)S(1)}, bf16[768,256]{0,1:T(8,128)(2,1)S(1)}, u32[]{:S(2)}, u32[]{:S(2)}) collective-permute-start(bf16[768,256]{0,1:T(8,128)(2,1)S(1)} %copy.98), channel_id=1, source_target_pairs={{0,0},{1,4},{2,8},{3,12},{4,1},{5,5},{6,9},{7,13},{8,2},{9,6},{10,... | collective-permute-start | bytes 1179656 | tf_op jit(solution)/shard_map/ppermute | solution.py:49
  49.4 78.8 %all-gather.9.cloned.1.call-start = ((), (), s32[]{:S(2)}) async-start(), calls=%async_computation.11 | async-start | bytes 3440640 | tf_op jit(solution)/shard_map/all_gather | solution.py:36
  50.9 115.6 %reduce-scatter.11.cloned.1.call-start = ((), (), s32[]{:S(2)}) async-start(), calls=%async_computation.12 | async-start | bytes 1966080 | tf_op jit(solution)/shard_map/reduce_scatter | solution.py:40
  63.0 26.4 %copy-start.11 = (bf16[768,576]{1,0:T(8,128)(2,1)}, bf16[768,576]{1,0:T(8,128)(2,1)S(1)}, u32[]{:S(2)}) copy-start(bf16[768,576]{1,0:T(8,128)(2,1)S(1)} %all_gather.23) | copy-start | bytes 2654212
  131.0 40.2 %copy-start.14 = (bf16[192,1024]{1,0:T(8,128)(2,1)S(1)}, bf16[192,1024]{1,0:T(8,128)(2,1)}, u32[]{:S(2)}) copy-start(bf16[192,1024]{1,0:T(8,128)(2,1)} %param.23) | copy-start | bytes 1179652
  131.0 100.2 %all-gather.11.cloned.1.call-start = ((), (), s32[]{:S(2)}) async-start(), calls=%async_computation.13 | async-start | bytes 1966080 | tf_op jit(solution)/shard_map/all_gather | solution.py:36
  171.1 99.2 %all-gather.13.cloned.1.call-start = ((), (), s32[]{:S(2)}) async-start(), calls=%async_computation.15 | async-start | bytes 1966080 | tf_op jit(solution)/shard_map/all_gather | solution.py:36
  181.0 49.2 %collective-permute-start.2 = (bf16[768,256]{0,1:T(8,128)(2,1)S(1)}, bf16[768,256]{0,1:T(8,128)(2,1)S(1)}, u32[]{:S(2)}, u32[]{:S(2)}) collective-permute-start(bf16[768,256]{0,1:T(8,128)(2,1)S(1)} %copy.110), channel_id=1, source_target_pairs={{0,0},{1,4},{2,8},{3,12},{4,1},{5,5},{6,9},{7,13},{8,2},{9,6},{10,... | collective-permute-start | bytes 1179656 | tf_op jit(solution)/shard_map/ppermute | solution.py:49
  230.1 0.7 copy-start.6
  230.9 39.4 %copy-start.23 = (f32[768]{0:T(1024)S(1)}, f32[768]{0:T(1024)}, u32[]{:S(2)}) copy-start(f32[768]{0:T(1024)} %param.21) | copy-start | bytes 9220
  230.9 85.7 %reduce-scatter.15.cloned.1.call-start = ((), (), s32[]{:S(2)}) async-start(), calls=%async_computation.16 | async-start | bytes 1966080 | tf_op jit(solution)/shard_map/reduce_scatter | solution.py:40
  276.9 1.1 copy-start.25
  282.2 34.5 %copy-start = (bf16[256,768]{1,0:T(8,128)(2,1)S(1)}, bf16[256,768]{1,0:T(8,128)(2,1)}, u32[]{:S(2)}) copy-start(bf16[256,768]{1,0:T(8,128)(2,1)} %reduce-scatter.11.cloned.1.call-done) | copy-start | bytes 1179652
  282.2 71.1 %reduce-scatter.13.cloned.1.call-start = ((), (), s32[]{:S(2)}) async-start(), calls=%async_computation.14 | async-start | bytes 1966080 | tf_op jit(solution)/shard_map/reduce_scatter | solution.py:40
  288.0 65.3 %copy-start.7 = (bf16[768,256]{0,1:T(8,128)(2,1)S(1)}, bf16[768,256]{0,1:T(8,128)(2,1)}, u32[]{:S(2)}) copy-start(bf16[768,256]{0,1:T(8,128)(2,1)} %copy-done.6) | copy-start | bytes 1179652
  288.0 104.1 %all-gather.15.cloned.1.call-start = ((), (), s32[]{:S(2)}) async-start(), calls=%async_computation.17 | async-start | bytes 1966080 | tf_op jit(solution)/shard_map/all_gather | solution.py:36
  356.1 104.6 %reduce-scatter.21.cloned.1.call-start = ((), (), s32[]{:S(2)}) async-start(), calls=%async_computation.21 | async-start | bytes 1228800
  397.8 1.0 copy-start.8
  399.4 0.8 copy-start.9
  402.4 1.0 copy-start.8
  404.0 0.8 copy-start.9
  404.8 2.6 copy-start.3
  406.4 2.1 copy-start.21
  407.4 1.1 copy-start.18
  408.5 2.5 copy-start.12
  410.9 77.8 %reduce-scatter.17.cloned.1.call-start = ((), (), s32[]{:S(2)}) async-start(), calls=%async_computation.18 | async-start | bytes 1966080 | tf_op jit(solution)/shard_map/reduce_scatter | solution.py:40
  414.8 3.9 copy-start.22
  414.9 116.4 %reduce-scatter.19.cloned.1.call-start = ((), (), s32[]{:S(2)}) async-start(), calls=%async_computation.20 | async-start | bytes 3440640
  415.2 3.6 copy-start.24
  418.8 2.0 copy-start.2
  425.8 1.0 copy-start.13
  426.8 29.5 %collective-permute-start.1 = (bf16[768,256]{0,1:T(8,128)(2,1)S(1)}, bf16[768,256]{0,1:T(8,128)(2,1)S(1)}, u32[]{:S(2)}, u32[]{:S(2)}) collective-permute-start(bf16[768,256]{0,1:T(8,128)(2,1)S(1)} %copy-done.13), channel_id=1, source_target_pairs={{0,0},{4,1},{8,2},{12,3},{1,4},{5,5},{9,6},{13,7},{2,8},{6,9},{10,... | collective-permute-start | bytes 1179656 | tf_op jit(solution)/shard_map/ppermute | solution.py:55
  457.2 81.6 %all-to-all-start.1 = ((bf16[4,192,256]{2,1,0:T(8,128)(2,1)}), bf16[4,192,256]{2,1,0:T(8,128)(2,1)S(1)}, u32[]{:S(2)}, u32[]{:S(2)}) async-start(bf16[4,192,256]{2,1,0:T(8,128)(2,1)} %bitcast.27), calls=%async_computation.3 | async-start | bytes 786432 | tf_op jit(solution)/shard_map/all_to_all | solution.py:56
  460.6 167.3 %all-reduce.3.cloned.1.call-start = ((), (), s32[]{:S(2)}) async-start(), calls=%async_computation.19 | async-start | bytes 2359296 | tf_op jit(solution)/shard_map/psum | solution.py:197
  490.2 44.7 %copy-start.5 = (f32[256,768]{1,0:T(8,128)S(1)}, f32[256,768]{1,0:T(8,128)}, u32[]{:S(2)}) copy-start(f32[256,768]{1,0:T(8,128)} %get-tuple-element.241) | copy-start | bytes 2359300
  490.2 44.8 %copy-start.10 = (bf16[256,768]{1,0:T(8,128)(2,1)S(1)}, bf16[256,768]{1,0:T(8,128)(2,1)}, u32[]{:S(2)}) copy-start(bf16[256,768]{1,0:T(8,128)(2,1)} %reduce-scatter.17.cloned.1.call-done) | copy-start | bytes 1179652
  534.9 35.1 %copy-start.4 = (bf16[2,512,3,64]{1,3,2,0:T(8,128)(2,1)S(1)}, bf16[2,512,3,64]{1,3,2,0:T(8,128)(2,1)}, u32[]{:S(2)}) copy-start(bf16[2,512,3,64]{1,3,2,0:T(8,128)(2,1)} %copy-done.3) | copy-start | bytes 1179652
  535.3 30.3 %collective-permute-start.3 = (bf16[768,256]{0,1:T(8,128)(2,1)S(1)}, bf16[768,256]{0,1:T(8,128)(2,1)S(1)}, u32[]{:S(2)}, u32[]{:S(2)}) collective-permute-start(bf16[768,256]{0,1:T(8,128)(2,1)S(1)} %fusion.90), channel_id=1, source_target_pairs={{0,0},{4,1},{8,2},{12,3},{1,4},{5,5},{9,6},{13,7},{2,8},{6,9},{10,... | collective-permute-start | bytes 1179656 | tf_op jit(solution)/shard_map/ppermute | solution.py:55
  566.5 60.7 %all-to-all-start.3 = ((bf16[4,192,256]{2,1,0:T(8,128)(2,1)}), bf16[4,192,256]{2,1,0:T(8,128)(2,1)S(1)}, u32[]{:S(2)}, u32[]{:S(2)}) async-start(bf16[4,192,256]{2,1,0:T(8,128)(2,1)} %bitcast.34), calls=%async_computation.7 | async-start | bytes 786432 | tf_op jit(solution)/shard_map/all_to_all | solution.py:56
  628.0 2.2 copy-start.1
Sparse Core Ops, SparseCore 0:
  49.5 37.2 all-gather.6
  88.7 39.4 all-gather.8
  131.1 35.4 reduce-scatter.10
  171.2 52.7 all-gather.10
  231.0 39.2 all-gather.12
  282.3 34.2 reduce-scatter.14
  318.9 34.2 reduce-scatter.12
  356.2 35.8 all-gather.14
  411.0 33.6 reduce-scatter.20
  446.9 41.8 reduce-scatter.16
  491.8 39.4 reduce-scatter.18
  535.0 19.9 all-reduce.2

commit v2 on v1

--- a/solution.py
+++ b/solution.py
@@ -1,6 +1,10 @@
+import functools
+
 import jax
 import jax.numpy as jnp
 from jax import lax
+from jax.experimental import pallas as pl
+from jax.experimental.pallas import tpu as pltpu
 from jax.sharding import PartitionSpec as P
 
 D = 768
@@ -32,28 +36,102 @@
     )
 
 
-def gather(local, axis_name):
+def swap_kernel(axis_name, count, shared, x_ref, o_ref, send_sem, recv_sem, own_sem):
+    me = lax.axis_index(axis_name)
+    barrier = pltpu.get_barrier_semaphore()
+    peers = [lax.rem(me + step, count) for step in range(1, count)]
+    for peer in peers:
+        pl.semaphore_signal(
+            barrier, inc=1, device_id={axis_name: peer}, device_id_type=pl.DeviceIdType.MESH
+        )
+    own = pltpu.make_async_copy(x_ref if shared else x_ref.at[me], o_ref.at[me], own_sem)
+    own.start()
+    pl.semaphore_wait(barrier, count - 1)
+    copies = []
+    for slot, peer in enumerate(peers):
+        copy = pltpu.make_async_remote_copy(
+            src_ref=x_ref if shared else x_ref.at[peer],
+            dst_ref=o_ref.at[me],
+            send_sem=send_sem.at[slot],
+            recv_sem=recv_sem.at[slot],
+            device_id={axis_name: peer},
+            device_id_type=pl.DeviceIdType.MESH,
+        )
+        copy.start()
+        copies.append(copy)
+    own.wait()
+    for copy in copies:
+        copy.wait()
+
+
+def swap(values, axis_name, shared, ident):
+    count = lax.axis_size(axis_name)
+    block = values.shape if shared else values.shape[1:]
+    moved = values.size * values.dtype.itemsize
+    return pl.pallas_call(
+        functools.partial(swap_kernel, axis_name, count, shared),
+        out_shape=jax.ShapeDtypeStruct((count, *block), values.dtype),
+        in_specs=[pl.BlockSpec(memory_space=pltpu.VMEM)],
+        out_specs=pl.BlockSpec(memory_space=pltpu.VMEM),
+        scratch_shapes=[
+            pltpu.SemaphoreType.DMA((count - 1,)),
+            pltpu.SemaphoreType.DMA((count - 1,)),
+            pltpu.SemaphoreType.DMA,
+        ],
+        compiler_params=pltpu.CompilerParams(collective_id=ident, has_side_effects=True),
+        cost_estimate=pl.CostEstimate(
+            flops=0, bytes_accessed=(20 if not shared else 60) * moved, transcendentals=0
+        ),
+    )(values)
+
+
+def gather_async(local, axis_name):
     return lax.all_gather(local, axis_name, axis=0, tiled=True)
 
 
-def scatter_sum(partial, axis_name):
+def scatter_sum_async(partial, axis_name):
     return lax.psum_scatter(
         partial.astype(jnp.bfloat16), axis_name, scatter_dimension=0, tiled=True
     ).astype(jnp.float32)
 
 
-def to_tokens(block):
+def gather(local, axis_name, ident):
+    return swap(local, axis_name, True, ident).reshape(-1, *local.shape[1:])
+
+
+def scatter_sum(partial, axis_name, ident):
+    count = lax.axis_size(axis_name)
+    pieces = partial.astype(jnp.bfloat16).reshape(count, -1, *partial.shape[1:])
+    return jnp.sum(swap(pieces, axis_name, False, ident).astype(jnp.float32), axis=0)
+
+
+def to_tokens(first, second, ident):
     rows, cols = lax.axis_size("row"), lax.axis_size("col")
-    block = lax.all_to_all(block, "row", split_axis=1, concat_axis=0, tiled=True)
+    share = first.shape[0]
+    block = jnp.concatenate([first.T, second.T], axis=1).reshape(rows, -1, 2 * share)
+    block = swap(block, "row", False, ident)
     moves = [(r * cols + c, c * rows + r) for r in range(rows) for c in range(cols)]
-    return lax.ppermute(block, ("row", "col"), moves).T
-
-
-def to_features(tokens):
+    block = lax.ppermute(block, ("row", "col"), moves)
+    first = jnp.concatenate([block[r, :, :share] for r in range(rows)], axis=1)
+    second = jnp.concatenate([block[r, :, share:] for r in range(rows)], axis=1)
+    return first, second
+
+
+def to_features(first, second, ident):
     rows, cols = lax.axis_size("row"), lax.axis_size("col")
+    share = first.shape[1] // rows
+    block = jnp.stack(
+        [
+            jnp.concatenate(
+                [first[:, r * share : (r + 1) * share], second[:, r * share : (r + 1) * share]], axis=1
+            )
+            for r in range(rows)
+        ]
+    )
     moves = [(c * rows + r, r * cols + c) for r in range(rows) for c in range(cols)]
-    block = lax.ppermute(tokens.T, ("row", "col"), moves)
-    return lax.all_to_all(block, "row", split_axis=0, concat_axis=1, tiled=True)
+    block = lax.ppermute(block, ("row", "col"), moves)
+    block = swap(block, "row", False, ident).reshape(-1, 2 * share)
+    return block[:, :share].T, block[:, share:].T
 
 
 def norm_forward(values, gain, bias):
@@ -127,19 +205,20 @@
     block_input, norm_gains, row_biases, w_qkv, qv_bias, w_out, w_up, up_bias, w_down, cotangent
 ):
     head_cols = w_qkv.shape[2]
-    inputs = to_tokens(block_input).astype(jnp.float32)
-    cot = to_tokens(cotangent)
-    vectors = gather(jnp.concatenate([norm_gains, row_biases], axis=0).T, "row").T
+    inputs, cot = to_tokens(block_input, cotangent, 0)
+    inputs = inputs.astype(jnp.float32)
+    vectors = swap(jnp.concatenate([norm_gains, row_biases], axis=0), "row", True, 1)
+    vectors = jnp.concatenate([vectors[r] for r in range(vectors.shape[0])], axis=1)
     gains, biases = vectors[:2], vectors[2:]
-    qkv_weight = gather(w_qkv.reshape(w_qkv.shape[0], -1), "row")
-    rest = gather(jnp.concatenate([w_out.T, w_up, w_down], axis=1), "row")
+    qkv_weight = gather_async(w_qkv.reshape(w_qkv.shape[0], -1), "row")
+    rest = gather_async(jnp.concatenate([w_out.T, w_up, w_down], axis=1), "row")
     width = w_up.shape[1]
     out_t = rest[:, :head_cols]
     up = rest[:, head_cols : head_cols + width]
     down = rest[:, head_cols + width :]
 
     normed_one, normal_one, inverse_one = norm_forward(inputs, gains[0], biases[0])
-    source_one = gather(normed_one.astype(jnp.bfloat16), "col")
+    source_one = gather(normed_one.astype(jnp.bfloat16), "col", 2)
     qkv_sum = multiply(source_one, qkv_weight, False)
     rows_here = qkv_sum.shape[0]
     qkv_sum = qkv_sum.reshape(rows_here, 3, head_cols)
@@ -149,16 +228,16 @@
     values_all = (qkv_sum[:, 2] + qv_bias[1]).astype(jnp.bfloat16).reshape(shape_four)
     attended, log_sums = attention_forward(queries, keys_all, values_all)
     attended_low = attended.reshape(rows_here, head_cols).astype(jnp.bfloat16)
-    middle = inputs + scatter_sum(multiply(attended_low, out_t, True), "col") + biases[2]
+    middle = inputs + scatter_sum(multiply(attended_low, out_t, True), "col", 3) + biases[2]
     normed_two, normal_two, inverse_two = norm_forward(middle, gains[1], biases[1])
-    source_two = gather(normed_two.astype(jnp.bfloat16), "col")
-    cot_all = gather(cot, "col")
+    source_two = gather(normed_two.astype(jnp.bfloat16), "col", 4)
+    cot_all = gather_async(cot, "col")
     before = multiply(source_two, up, False) + up_bias
     hidden_low = gelu_tanh(before).astype(jnp.bfloat16)
     grad_hidden = multiply(cot_all, down, False)
     grad_before = jax.vjp(gelu_tanh, before)[1](grad_hidden)[0].astype(jnp.bfloat16)
-    grad_normed_two = scatter_sum(multiply(grad_before, up, True), "col")
-    output = middle + scatter_sum(multiply(hidden_low, down, True), "col") + biases[3]
+    grad_normed_two = scatter_sum(multiply(grad_before, up, True), "col", 5)
+    output = middle + scatter_sum_async(multiply(hidden_low, down, True), "col") + biases[3]
     grad_w_down = contract_tokens(cot_all, hidden_low)
     grad_up_bias = jnp.sum(grad_before.astype(jnp.float32), axis=0)
     grad_w_up = contract_tokens(source_two, grad_before)
@@ -170,7 +249,7 @@
     grad_middle_low = grad_middle.astype(jnp.bfloat16)
     grad_out_bias = jnp.sum(grad_middle_low.astype(jnp.float32), axis=0)
     grad_down_bias = jnp.sum(grad_out, axis=0)
-    grad_middle_all = gather(grad_middle_low, "col")
+    grad_middle_all = gather(grad_middle_low, "col", 6)
     grad_att_low = multiply(grad_middle_all, out_t, False).astype(jnp.bfloat16).reshape(shape_four)
     grad_w_out_t = contract_tokens(grad_middle_all, attended_low)
     grad_q, grad_k, grad_v = attention_backward(
@@ -183,32 +262,41 @@
     grad_qv = jnp.stack(
         [jnp.sum(grad_q.astype(jnp.float32), axis=0), jnp.sum(grad_v.astype(jnp.float32), axis=0)]
     )
-    grad_normed_one = scatter_sum(multiply(grad_qkv_low, qkv_weight, True), "col")
+    grad_normed_one = scatter_sum(multiply(grad_qkv_low, qkv_weight, True), "col", 7)
     grad_w_qkv = contract_tokens(source_one, grad_qkv_low)
     back_one, gain_one, shift_one = norm_backward(
         grad_normed_one, gains[0], normal_one, inverse_one
     )
     grad_input = grad_middle + back_one
 
-    mlp_sum = scatter_sum(
-        jnp.concatenate([grad_w_out_t, grad_w_up, grad_w_down], axis=1), "row"
-    )
-    qkv_grad = scatter_sum(grad_w_qkv, "row")
-    weights_sum = lax.psum(
-        jnp.concatenate([mlp_sum, qkv_grad], axis=1).astype(jnp.bfloat16), "dp"
-    ).astype(jnp.float32)
-    sum_out = weights_sum[:, :head_cols].T
-    sum_up = weights_sum[:, head_cols : head_cols + width]
-    sum_down = weights_sum[:, head_cols + width : head_cols + 2 * width]
-    sum_qkv = weights_sum[:, head_cols + 2 * width :].reshape(w_qkv.shape)
-    small = jnp.stack([gain_one, gain_two, shift_one, shift_two, grad_out_bias, grad_down_bias])
-    small = lax.psum(small, ("dp", "row", "col"))
+    mlp_sum = scatter_sum_async(jnp.concatenate([grad_w_up, grad_w_down], axis=1), "row")
+    mlp_sum = lax.psum(mlp_sum.astype(jnp.bfloat16), "dp").astype(jnp.float32)
+    att_sum = scatter_sum(jnp.concatenate([grad_w_qkv, grad_w_out_t], axis=1), "row", 8)
+    att_sum = jnp.sum(
+        swap(att_sum.astype(jnp.bfloat16), "dp", True, 9).astype(jnp.float32), axis=0
+    )
+    sum_up = mlp_sum[:, :width]
+    sum_down = mlp_sum[:, width:]
+    sum_qkv = att_sum[:, : 3 * head_cols].reshape(w_qkv.shape)
+    sum_out = att_sum[:, 3 * head_cols :].T
+    features = gains.shape[1]
+    longest = max(features, width, 2 * head_cols)
+    small = [gain_one, gain_two, shift_one, shift_two, grad_out_bias, grad_down_bias]
+    small = small + [grad_up_bias, grad_qv.reshape(-1)]
+    small = jnp.stack([jnp.pad(row, (0, longest - row.shape[0])) for row in small])
+    small = jnp.sum(swap(small, "dp", True, 10), axis=0)
+    small = jnp.sum(swap(small, "row", True, 11), axis=0)
+    sum_upb = small[6, :width]
+    sum_qv = small[7, : 2 * head_cols].reshape(2, head_cols)
     share = norm_gains.shape[1]
-    small = lax.dynamic_slice_in_dim(small, lax.axis_index("row") * share, share, axis=1)
-    sum_qv, sum_upb = lax.psum((grad_qv, grad_up_bias), ("dp", "row"))
+    small = lax.dynamic_slice_in_dim(small[:6], lax.axis_index("row") * share, share, axis=1)
+    small = jnp.sum(swap(small, "col", True, 12), axis=0)
+    output_t, grad_input_t = to_features(
+        output.astype(jnp.bfloat16), grad_input.astype(jnp.bfloat16), 13
+    )
     return (
-        to_features(output.astype(jnp.bfloat16)),
-        to_features(grad_input.astype(jnp.bfloat16)),
+        output_t,
+        grad_input_t,
         small[:2],
         small[2:],
         sum_qkv,

time: 650 us -> 569 us (0.88)
  waiting for transfers between devices: 402 us -> 10.6 us
  Pallas kernels: 0 us -> 368 us
  blocking collectives: 99.9 us -> 16.1 us
  local copies, waits for them, and re-layouts: 32.2 us -> 48.6 us
  other arithmetic: 19.6 us -> 34 us
    pallas_call x0 -> x14, Pallas kernels: none -> 368 us  [swap(): pl.pallas_call(functools.partial(swap_kernel, axis_name, count, shared),...]
    reduce_scatter x4 -> x1, waiting for transfers between devices: 125 us -> 0.02 us  [scatter_sum_async(): lax.psum_scatter(partial.astype(jnp.bfloat16), axis_name, scatter_dimensi...]
    all_gather x5 -> x2, waiting for transfers between devices: 124 us -> 0.02 us  [gather_async(): return lax.all_gather(local, axis_name, axis=0, tiled=True)]
    ppermute x4 -> x2, waiting for transfers between devices: 111 us -> 10.5 us  [the longest x1 10.5 us: to_tokens(): block = lax.ppermute(block, ('row', 'col'), moves)]
    psum x2 -> x0, blocking collectives: 55.5 us -> none  [the longest x1 40.5 us: body(): small = lax.psum(small, ('dp', 'row', 'col'))]
    unnamed x14 -> x6, waiting for transfers between devices: 41.3 us -> 0.1 us
    all_to_all x2 -> x0, blocking collectives: 19.7 us -> none  [to_tokens(): lax.all_to_all(block, 'row', split_axis=1, concat_axis=0, tiled=True)]
    reduce_sum x0 -> x7, other arithmetic: none -> 9.85 us  [the longest x2 4.03 us: scatter_sum(): jnp.sum(swap(pieces, axis_name, False, ident).astype(jnp.float32), axis=0)]
  transfers between devices with their start and end apart: 18 -> 7, of which waited for: 13 -> 1; matrix products, arithmetic and copies ran while one was open for 8% -> 21% of each run, Pallas kernels for 0% -> 63%
where the time goes in v2:
time: 569 us; the launch traced here: 562 us
  Pallas kernels  368 us (65%)
  local copies, waits for them, and re-layouts  48.6 us (9%)
  matrix products  47.6 us (8%)
  other arithmetic  34 us (6%)
  starting transfers between devices  22.2 us (4%)
  blocking collectives  16.1 us (3%)
  between operations  15.2 us (3%)
  waiting for transfers between devices  10.6 us (2%)
    pallas_call x14, Pallas kernels, swap(): pl.pallas_call(functools.partial(swap_kernel, axis_name, count, shared),...  368 us
    unnamed x124, local copies, waits for them, and re-layouts  18.7 us
    all_gather x1, blocking collectives, gather_async(): return lax.all_gather(local, axis_name, axis=0, tiled=True)  16.1 us
    dot_general x4, matrix products, multiply(): lax.dot_general(rows, weight, (((1,), (1,)), ((), ())), preferred_element...  15.4 us
    dot_general x4, matrix products, multiply(): return jnp.dot(rows, weight, preferred_element_type=jnp.float32)  15.3 us
  transfers between devices with their start and end apart: 7, of which 1 were waited for; matrix products, arithmetic and copies ran while one was open for 21% of the time, Pallas kernels for 63%

profile of v2, /device:TPU:2, one launch (start us, length us, event | category | flops | bytes accessed | tf_op | source)
XLA Modules:
  0.0 562.4 jit_solution(15469994032200159057)
XLA Ops:
  7.3 1.2 pad_maximum_fusion.2
  8.5 1.2 copy.67
  9.7 13.9 %shard_map.177 = bf16[4,256,384]{2,1,0:T(8,128)(2,1)} custom-call(bf16[4,256,384]{2,1,0:T(8,128)(2,1)} %bitcast.218), custom_call_target="tpu_custom_call" | custom-call | bytes 15728640 | tf_op jit(solution)/shard_map/pallas_call | solution.py:71
  23.6 3.5 collective-permute-start
  27.3 1.3 concatenate.46
  29.3 19.7 %shard_map.178 = f32[4,6,192]{2,1,0:T(8,128)} custom-call(f32[6,192]{1,0:T(8,128)} %pad_maximum_fusion.6.x_ref), custom_call_target="tpu_custom_call" | custom-call | bytes 276480 | tf_op jit(solution)/shard_map/pallas_call | solution.py:71
  49.4 16.1 %all_gather.9 = bf16[768,576]{1,0:T(8,128)(2,1)S(1)} all-gather(bf16[192,576]{1,0:T(8,128)(2,1)S(1)} %copy.69), channel_id=1, replica_groups=mesh['dp'=2,'row'=4,'col'=4] {'row'}, dimensions={0}, use_global_device_ids=true | all-gather | bytes 1105920 | tf_op jit(solution)/shard_map/all_gather | solution.py:89
  68.3 10.5 %collective-permute-done = bf16[4,256,384]{2,1,0:T(8,128)(2,1)S(1)} collective-permute-done((bf16[4,256,384]{2,1,0:T(8,128)(2,1)}, bf16[4,256,384]{2,1,0:T(8,128)(2,1)S(1)}, u32[]{:S(2)}, u32[]{:S(2)}) %collective-permute-start) | collective-permute-done | bytes 786464 | tf_op jit(solution)/shard_map/ppermute | solution.py:114
  81.2 32.9 %shard_map.179 = bf16[4,256,768]{2,1,0:T(8,128)(2,1)} custom-call(bf16[256,768]{1,0:T(8,128)(2,1)} %fusion.70.x_ref), custom_call_target="tpu_custom_call" | custom-call | bytes 23592960 | tf_op jit(solution)/shard_map/pallas_call | solution.py:71
  114.2 2.5 fusion.91
  119.7 5.4 while.26
  121.3 1.1 fusion.127
  124.0 1.1 fusion.127
  126.3 1.5 convert_reduce_fusion.8
  128.2 2.8 convolution_convert_fusion.3
  131.0 56.0 %shard_map.180 = bf16[4,256,768]{2,1,0:T(8,128)(2,1)} custom-call(bf16[4,256,768]{2,1,0:T(8,128)(2,1)} %bitcast.212), custom_call_target="tpu_custom_call" | custom-call | bytes 31457280 | tf_op jit(solution)/shard_map/pallas_call | solution.py:71
  187.0 1.7 convert_reduce_fusion.5
  190.2 45.1 %shard_map.181 = bf16[4,256,768]{2,1,0:T(8,128)(2,1)} custom-call(bf16[256,768]{1,0:T(8,128)(2,1)} %add_convert_fusion.1.x_ref), custom_call_target="tpu_custom_call" | custom-call | bytes 23592960 | tf_op jit(solution)/shard_map/pallas_call | solution.py:71
  235.2 3.3 fusion.61
  238.6 1.7 copy-done.54
  240.3 4.8 convolution_convert_fusion.2
  245.1 2.1 reshape.193
  247.2 1.7 copy.83
  248.9 1.3 stack.61
  250.2 7.3 %convert_reduce_fusion.4 = (f32[768]{0:T(1024)}, bf16[1024,768]{1,0:T(8,128)(2,1)S(1)}) fusion(bf16[1024,768]{1,0:T(8,128)(2,1)} %all-gather.5.cloned.1.call-done, bf16[768,1728]{1,0:T(8,128)(2,1)} %all-gather.3.cloned.1.call-done, f32[1024,768]{1,0:T(8,128)} %copy-done.54, f32[768]{0:T(1024)} %param.21), kind=kOutput, calls=%fused_computation.70 | convolution fusion | flops 1229192448 | bytes 7478272 | tf_op jit(solution)/shard_map/dot_general | solution.py:30
  257.5 1.2 copy-done.56
  258.7 1.4 convolution_convert_fusion.5
  261.1 2.0 convolution_convert_fusion.4
  263.1 1.6 pad_maximum_fusion
  264.6 4.4 copy.94
  269.0 4.0 convolution_convert_fusion.1
  273.0 44.4 %shard_map.182 = bf16[4,256,768]{2,1,0:T(8,128)(2,1)} custom-call(bf16[4,256,768]{2,1,0:T(8,128)(2,1)} %bitcast.223), custom_call_target="tpu_custom_call" | custom-call | bytes 31457280 | tf_op jit(solution)/shard_map/pallas_call | solution.py:71
  317.5 2.1 convert_reduce_fusion.2
  320.8 8.2 %all-reduce.3.cloned.1.call-start = ((), (), s32[]{:S(2)}) async-start(), calls=%async_computation.5 | async-start | bytes 1572864 | tf_op jit(solution)/shard_map/psum | solution.py:273
  329.0 2.7 multiply_reduce_fusion.1
  331.7 1.9 convert_reduce_fusion.11
  333.6 39.2 %shard_map.183 = bf16[4,256,768]{2,1,0:T(8,128)(2,1)} custom-call(bf16[256,768]{1,0:T(8,128)(2,1)} %get-tuple-element.223.x_ref), custom_call_target="tpu_custom_call" | custom-call | bytes 23592960 | tf_op jit(solution)/shard_map/pallas_call | solution.py:71
  372.9 2.2 convolution_convert_fusion.8
  377.7 11.5 %while.27 = (s32[]{:T(128)}, bf16[2,512,3,64]{1,3,2,0:T(8,128)(2,1)}, bf16[2,512,3,64]{1,3,2,0:T(8,128)(2,1)}, bf16[2,512,3,64]{1,3,2,0:T(8,128)(2,1)}, bf16[2,5...) while((s32[]{:T(128)}, ...), condition=%wide.region_15.16_spmd, body=%wide.region_13.15_spmd.sunk | while | flops 510851584 | bytes 33002712 | solution.py:201
  382.2 1.3 fusion.138
  387.9 1.3 fusion.138
  389.2 1.6 copy.84
  391.8 1.5 copy.80
  395.1 1.4 convolution_convert_fusion.6
  396.6 1.2 pad_maximum_fusion.1.x_ref
  397.8 16.8 %shard_map.189 = bf16[4,192,768]{2,1,0:T(8,128)(2,1)} custom-call(bf16[4,192,768]{2,1,0:T(8,128)(2,1)} %pad_maximum_fusion.1.x_ref), custom_call_target="tpu_custom_call" | custom-call | bytes 23592960 | tf_op jit(solution)/shard_map/pallas_call | solution.py:71
  414.6 2.3 reduce_sum.269.x_ref
  416.9 3.4 shard_map.190
  420.3 1.2 convert_reduce_fusion.7
  421.8 3.9 convolution_convert_fusion
  425.7 40.2 %shard_map.184 = bf16[4,256,768]{2,1,0:T(8,128)(2,1)} custom-call(bf16[4,256,768]{2,1,0:T(8,128)(2,1)} %bitcast.222), custom_call_target="tpu_custom_call" | custom-call | bytes 31457280 | tf_op jit(solution)/shard_map/pallas_call | solution.py:71
  465.9 2.1 convert_reduce_fusion
  469.8 10.1 %collective-permute-start.1 = (bf16[4,256,384]{2,1,0:T(8,128)(2,1)S(1)}, bf16[4,256,384]{2,1,0:T(8,128)(2,1)}, u32[]{:S(2)}, u32[]{:S(2)}) collective-permute-start(bf16[4,256,384]{2,1,0:T(8,128)(2,1)S(1)} %pad_maximum_fusion.3), channel_id=1, source_target_pairs={{0,0},{4,1},{8,2},{12,3},{1,4},{5,5},{9,6},{13,7},{2,8},{6,9},{10,... | collective-permute-start | bytes 2359304 | tf_op jit(solution)/shard_map/ppermute | solution.py:132
  479.9 1.1 convert_reduce_fusion.9
  481.9 2.6 shard_map.186
  484.5 1.4 reduce_sum.266.x_ref
  485.9 14.1 %shard_map.187 = f32[4,8,768]{2,1,0:T(8,128)} custom-call(f32[8,768]{1,0:T(8,128)} %reduce_sum.266.x_ref), custom_call_target="tpu_custom_call" | custom-call | bytes 1474560 | tf_op jit(solution)/shard_map/pallas_call | solution.py:71
  501.1 2.2 copy.95
  504.0 22.9 %shard_map.188 = f32[4,6,192]{2,1,0:T(8,128)} custom-call(f32[6,192]{1,0:T(8,128)} %constant_dynamic-slice_fusion.x_ref), custom_call_target="tpu_custom_call" | custom-call | bytes 276480 | tf_op jit(solution)/shard_map/pallas_call | solution.py:71
  529.1 1.1 copy.86
  532.3 16.7 %shard_map.185 = bf16[4,256,384]{2,1,0:T(8,128)(2,1)} custom-call(bf16[4,256,384]{2,1,0:T(8,128)(2,1)} %collective-permute-done.1.x_ref), custom_call_target="tpu_custom_call" | custom-call | bytes 15728640 | tf_op jit(solution)/shard_map/pallas_call | solution.py:71
  549.0 1.5 fusion.88
  552.3 1.2 fusion.87
  553.6 1.1 copy.88
  (248 shorter events, 43.4 us)
Async XLA Ops:
  7.2 19.9 %copy-start.26 = (bf16[192,192]{1,0:T(8,128)(2,1)S(1)}, bf16[192,192]{1,0:T(8,128)(2,1)}, u32[]{:S(2)}) copy-start(bf16[192,192]{1,0:T(8,128)(2,1)} %param.19) | copy-start | bytes 221188
  7.2 20.1 %copy-start.22 = (bf16[192,768]{1,0:T(8,128)(2,1)S(1)}, bf16[192,768]{1,0:T(8,128)(2,1)}, u32[]{:S(2)}) copy-start(bf16[192,768]{1,0:T(8,128)(2,1)} %param.20) | copy-start | bytes 884740
  7.2 20.1 %copy-start.23 = (bf16[192,768]{1,0:T(8,128)(2,1)S(1)}, bf16[192,768]{1,0:T(8,128)(2,1)}, u32[]{:S(2)}) copy-start(bf16[192,768]{1,0:T(8,128)(2,1)} %param.22) | copy-start | bytes 884740
  7.2 121.0 %all-gather.3.cloned.1.call-start = ((), (), s32[]{:S(2)}) async-start(), calls=%async_computation.2 | async-start | bytes 3440640 | tf_op jit(solution)/shard_map/all_gather | solution.py:89
  8.5 20.2 %copy-start.47 = (f32[4,192]{1,0:T(4,128)S(1)}, f32[4,192]{1,0:T(4,128)}, u32[]{:S(2)}) copy-start(f32[4,192]{1,0:T(4,128)} %param.16) | copy-start | bytes 9220
  8.5 20.2 %copy-start.49 = (f32[2,192]{1,0:T(2,128)S(1)}, f32[2,192]{1,0:T(2,128)}, u32[]{:S(2)}) copy-start(f32[2,192]{1,0:T(2,128)} %param.15) | copy-start | bytes 4612
  8.5 40.5 %copy-start.21 = (bf16[192,3,192]{2,0,1:T(8,128)(2,1)S(1)}, bf16[192,3,192]{2,0,1:T(8,128)(2,1)}, u32[]{:S(2)}) copy-start(bf16[192,3,192]{2,0,1:T(8,128)(2,1)} %param.17) | copy-start | bytes 663556
  23.6 55.2 %collective-permute-start = (bf16[4,256,384]{2,1,0:T(8,128)(2,1)}, bf16[4,256,384]{2,1,0:T(8,128)(2,1)S(1)}, u32[]{:S(2)}, u32[]{:S(2)}) collective-permute-start(bf16[4,256,384]{2,1,0:T(8,128)(2,1)} %shard_map.177), channel_id=1, source_target_pairs={{0,0},{1,4},{2,8},{3,12},{4,1},{5,5},{6,9},{7,13},{8,2},{9,6},{10,... | collective-permute-start | bytes 2359304 | tf_op jit(solution)/shard_map/ppermute | solution.py:114
  28.6 37.5 %copy-start.50 = (f32[2,192]{1,0:T(2,128)S(1)}, f32[2,192]{1,0:T(2,128)}, u32[]{:S(2)}) copy-start(f32[2,192]{1,0:T(2,128)} %param.18) | copy-start | bytes 4612
  28.6 221.6 %all-gather.5.cloned.1.call-start = ((), (), s32[]{:S(2)}) async-start(), calls=%async_computation.4 | async-start | bytes 1966080 | tf_op jit(solution)/shard_map/all_gather | solution.py:89
  49.0 18.4 %copy-start.25 = (f32[4,6,192]{2,1,0:T(8,128)S(1)}, f32[4,6,192]{2,1,0:T(8,128)}, u32[]{:S(2)}) copy-start(f32[4,6,192]{2,1,0:T(8,128)} %shard_map.178) | copy-start | bytes 55300
  65.5 15.7 %copy-start.4 = (bf16[768,576]{1,0:T(8,128)(2,1)}, bf16[768,576]{1,0:T(8,128)(2,1)S(1)}, u32[]{:S(2)}) copy-start(bf16[768,576]{1,0:T(8,128)(2,1)S(1)} %all_gather.9) | copy-start | bytes 2654212
  67.6 46.6 %copy-start.27 = (f32[768]{0:T(1024)}, f32[768]{0:T(1024)S(1)}, u32[]{:S(2)}) copy-start(f32[768]{0:T(1024)S(1)} %get-tuple-element.186) | copy-start | bytes 9220
  79.9 36.8 %copy-start.31 = (f32[256]{0:T(256)}, f32[256]{0:T(256)S(1)}, u32[]{:S(2)}) copy-start(f32[256]{0:T(256)S(1)} %broadcast_multiply_fusion.5) | copy-start | bytes 3076
  80.2 36.5 %copy-start.35 = (f32[256]{0:T(256)}, f32[256]{0:T(256)S(1)}, u32[]{:S(2)}) copy-start(f32[256]{0:T(256)S(1)} %add_rsqrt_fusion.1) | copy-start | bytes 3076
  119.7 6.6 %copy-start.19 = (bf16[256,192]{1,0:T(8,128)(2,1)S(1)}, bf16[256,192]{1,0:T(8,128)(2,1)}, u32[]{:S(2)}) copy-start(bf16[256,192]{1,0:T(8,128)(2,1)} %get-tuple-element.243) | copy-start | bytes 294916
  125.1 61.9 %copy-start.2 = (bf16[2,512,3,64]{1,3,2,0:T(8,128)(2,1)}, bf16[2,512,3,64]{1,3,2,0:T(8,128)(2,1)S(1)}, u32[]{:S(2)}) copy-start(bf16[2,512,3,64]{1,3,2,0:T(8,128)(2,1)S(1)} %get-tuple-element.424) | copy-start | bytes 1179652
  127.8 201.1 %reduce-scatter.5.cloned.1.call-start = ((), (), s32[]{:S(2)}) async-start(), calls=%async_computation.3 | async-start | bytes 1966080 | tf_op jit(solution)/shard_map/reduce_scatter | solution.py:93
  131.0 57.7 %copy-start.41 = (f32[768]{0:T(1024)S(1)}, f32[768]{0:T(1024)}, u32[]{:S(2)}) copy-start(f32[768]{0:T(1024)} %get-tuple-element.185) | copy-start | bytes 9220
  187.0 2.2 copy-start.29
  187.0 2.2 copy-start.40
  188.9 49.6 %copy-start.33 = (f32[256]{0:T(256)}, f32[256]{0:T(256)S(1)}, u32[]{:S(2)}) copy-start(f32[256]{0:T(256)S(1)} %broadcast_multiply_fusion.4) | copy-start | bytes 3076
  189.2 49.4 %copy-start.37 = (f32[256]{0:T(256)}, f32[256]{0:T(256)S(1)}, u32[]{:S(2)}) copy-start(f32[256]{0:T(256)S(1)} %add_rsqrt_fusion) | copy-start | bytes 3076
  235.2 5.0 copy-start.52
  238.6 1.7 copy-start.54
  245.0 2.2 copy-start.1
  245.1 256.1 %reduce-scatter.7.cloned.1.call-start = ((), (), s32[]{:S(2)}) async-start(), calls=%async_computation.6 | async-start | bytes 2949120
  250.2 8.5 %copy-start.18 = (bf16[4,256,768]{2,1,0:T(8,128)(2,1)S(1)}, bf16[4,256,768]{2,1,0:T(8,128)(2,1)}, u32[]{:S(2)}) copy-start(bf16[4,256,768]{2,1,0:T(8,128)(2,1)} %shard_map.181) | copy-start | bytes 4718596
  257.5 1.2 copy-start.56
  258.7 1.5 copy-start.51
  258.7 1.5 copy-start.53
  258.7 2.4 copy-start.55
  264.6 4.4 copy-start.57
  273.0 47.1 %copy-start.48 = (f32[768]{0:T(1024)S(1)}, f32[768]{0:T(1024)}, u32[]{:S(2)}) copy-start(f32[768]{0:T(1024)} %get-tuple-element.260) | copy-start | bytes 9220
  317.4 11.5 %copy-start.30 = (f32[768]{0:T(1024)S(1)}, f32[768]{0:T(1024)}, u32[]{:S(2)}) copy-start(f32[768]{0:T(1024)} %get-tuple-element.184) | copy-start | bytes 9220
  317.5 11.5 %copy-start.34 = (f32[256]{0:T(256)S(1)}, f32[256]{0:T(256)}, u32[]{:S(2)}) copy-start(f32[256]{0:T(256)} %copy-done.33) | copy-start | bytes 3076
  317.5 11.5 %copy-start.38 = (f32[256]{0:T(256)S(1)}, f32[256]{0:T(256)}, u32[]{:S(2)}) copy-start(f32[256]{0:T(256)} %copy-done.37) | copy-start | bytes 3076
  317.5 11.5 %copy-start.39 = (f32[768]{0:T(1024)S(1)}, f32[768]{0:T(1024)}, u32[]{:S(2)}) copy-start(f32[768]{0:T(1024)} %get-tuple-element.182) | copy-start | bytes 9220
  319.6 12.1 %copy-start.6 = (bf16[256,768]{1,0:T(8,128)(2,1)S(1)}, bf16[256,768]{1,0:T(8,128)(2,1)}, u32[]{:S(2)}) copy-start(bf16[256,768]{1,0:T(8,128)(2,1)} %get-tuple-element.221) | copy-start | bytes 1179652
  320.8 231.5 %all-reduce.3.cloned.1.call-start = ((), (), s32[]{:S(2)}) async-start(), calls=%async_computation.5 | async-start | bytes 1572864 | tf_op jit(solution)/shard_map/psum | solution.py:273
  372.9 4.9 copy-start.3
  377.7 11.5 %copy-start = (bf16[4,256,768]{2,1,0:T(8,128)(2,1)S(1)}, bf16[4,256,768]{2,1,0:T(8,128)(2,1)}, u32[]{:S(2)}) copy-start(bf16[4,256,768]{2,1,0:T(8,128)(2,1)} %shard_map.183) | copy-start | bytes 4718596
  379.4 1.6 copy-start.8
  381.0 1.2 copy-start.16
  385.2 1.6 copy-start.8
  386.8 1.2 copy-start.16
  389.2 1.6 copy-start.10
  389.2 2.1 copy-start.17
  391.3 2.2 copy-start.14
  391.3 2.2 copy-start.20
  393.3 1.8 copy-start.13
  393.5 3.1 copy-start.24
  414.6 7.2 %copy-start.5 = (bf16[768,576]{1,0:T(8,128)(2,1)S(1)}, bf16[768,576]{1,0:T(8,128)(2,1)}, u32[]{:S(2)}) copy-start(bf16[768,576]{1,0:T(8,128)(2,1)} %copy-done.4) | copy-start | bytes 2654212
  425.7 42.3 %copy-start.28 = (f32[768]{0:T(1024)S(1)}, f32[768]{0:T(1024)}, u32[]{:S(2)}) copy-start(f32[768]{0:T(1024)} %copy-done.27) | copy-start | bytes 9220
  425.7 42.3 %copy-start.32 = (f32[256]{0:T(256)S(1)}, f32[256]{0:T(256)}, u32[]{:S(2)}) copy-start(f32[256]{0:T(256)} %copy-done.31) | copy-start | bytes 3076
  425.7 42.3 %copy-start.36 = (f32[256]{0:T(256)S(1)}, f32[256]{0:T(256)}, u32[]{:S(2)}) copy-start(f32[256]{0:T(256)} %copy-done.35) | copy-start | bytes 3076
  425.7 42.8 %copy-start.11 = (f32[256,768]{1,0:T(8,128)S(1)}, f32[256,768]{1,0:T(8,128)}, u32[]{:S(2)}) copy-start(f32[256,768]{1,0:T(8,128)} %get-tuple-element.224) | copy-start | bytes 2359300
  468.0 1.0 copy-start.12
  468.8 12.4 %copy-start.43 = (f32[768]{0:T(1024)S(1)}, f32[768]{0:T(1024)}, u32[]{:S(2)}) copy-start(f32[768]{0:T(1024)} %get-tuple-element.222) | copy-start | bytes 9220
  468.8 12.4 %copy-start.42 = (f32[768]{0:T(1024)S(1)}, f32[768]{0:T(1024)}, u32[]{:S(2)}) copy-start(f32[768]{0:T(1024)} %get-tuple-element.172) | copy-start | bytes 9220
  468.8 12.4 %copy-start.44 = (f32[1,768]{1,0:T(1,128)S(1)}, f32[1,768]{1,0:T(1,128)}, u32[]{:S(2)}) copy-start(f32[1,768]{1,0:T(1,128)} %stack.61) | copy-start | bytes 9220
  468.9 12.4 %copy-start.45 = (f32[1,768]{1,0:T(1,128)S(1)}, f32[1,768]{1,0:T(1,128)}, u32[]{:S(2)}) copy-start(f32[1,768]{1,0:T(1,128)} %stack.59) | copy-start | bytes 9220
  468.9 12.4 %copy-start.46 = (f32[1,768]{1,0:T(1,128)S(1)}, f32[1,768]{1,0:T(1,128)}, u32[]{:S(2)}) copy-start(f32[1,768]{1,0:T(1,128)} %stack.62) | copy-start | bytes 9220
  469.8 62.5 %collective-permute-start.1 = (bf16[4,256,384]{2,1,0:T(8,128)(2,1)S(1)}, bf16[4,256,384]{2,1,0:T(8,128)(2,1)}, u32[]{:S(2)}, u32[]{:S(2)}) collective-permute-start(bf16[4,256,384]{2,1,0:T(8,128)(2,1)S(1)} %pad_maximum_fusion.3), channel_id=1, source_target_pairs={{0,0},{4,1},{8,2},{12,3},{1,4},{5,5},{9,6},{13,7},{2,8},{6,9},{10,... | collective-permute-start | bytes 2359304 | tf_op jit(solution)/shard_map/ppermute | solution.py:132
  (5 other events, 4.2 us)
Sparse Core Ops, SparseCore 0:
  28.7 68.5 all-gather.2
  128.0 68.6 all-gather.4
  245.2 58.5 reduce-scatter.4
  320.9 44.5 reduce-scatter.6
  503.5 34.3 all-reduce.2

commit v3 on v2

--- a/solution.py
+++ b/solution.py
@@ -110,8 +110,9 @@
     share = first.shape[0]
     block = jnp.concatenate([first.T, second.T], axis=1).reshape(rows, -1, 2 * share)
     block = swap(block, "row", False, ident)
-    moves = [(r * cols + c, c * rows + r) for r in range(rows) for c in range(cols)]
-    block = lax.ppermute(block, ("row", "col"), moves)
+    if rows != cols:
+        moves = [(r * cols + c, c * rows + r) for r in range(rows) for c in range(cols)]
+        block = lax.ppermute(block, ("row", "col"), moves)
     first = jnp.concatenate([block[r, :, :share] for r in range(rows)], axis=1)
     second = jnp.concatenate([block[r, :, share:] for r in range(rows)], axis=1)
     return first, second
@@ -128,10 +129,19 @@
             for r in range(rows)
         ]
     )
-    moves = [(c * rows + r, r * cols + c) for r in range(rows) for c in range(cols)]
-    block = lax.ppermute(block, ("row", "col"), moves)
+    if rows != cols:
+        moves = [(c * rows + r, r * cols + c) for r in range(rows) for c in range(cols)]
+        block = lax.ppermute(block, ("row", "col"), moves)
     block = swap(block, "row", False, ident).reshape(-1, 2 * share)
     return block[:, :share].T, block[:, share:].T
+
+
+def flip(block):
+    rows, cols = lax.axis_size("row"), lax.axis_size("col")
+    if rows != cols:
+        return block
+    moves = [(r * cols + c, c * rows + r) for r in range(rows) for c in range(cols)]
+    return lax.ppermute(block, ("row", "col"), moves)
 
 
 def norm_forward(values, gain, bias):
@@ -205,20 +215,23 @@
     block_input, norm_gains, row_biases, w_qkv, qv_bias, w_out, w_up, up_bias, w_down, cotangent
 ):
     head_cols = w_qkv.shape[2]
+    square = lax.axis_size("row") == lax.axis_size("col")
+    heads_axis, split_axis = ("row", "col") if square else ("col", "row")
+    qv_bias, up_bias = flip(qv_bias), flip(up_bias)
     inputs, cot = to_tokens(block_input, cotangent, 0)
     inputs = inputs.astype(jnp.float32)
     vectors = swap(jnp.concatenate([norm_gains, row_biases], axis=0), "row", True, 1)
     vectors = jnp.concatenate([vectors[r] for r in range(vectors.shape[0])], axis=1)
     gains, biases = vectors[:2], vectors[2:]
-    qkv_weight = gather_async(w_qkv.reshape(w_qkv.shape[0], -1), "row")
-    rest = gather_async(jnp.concatenate([w_out.T, w_up, w_down], axis=1), "row")
+    qkv_weight = gather_async(flip(w_qkv.reshape(w_qkv.shape[0], -1)), split_axis)
+    rest = gather_async(flip(jnp.concatenate([w_out.T, w_up, w_down], axis=1)), split_axis)
     width = w_up.shape[1]
     out_t = rest[:, :head_cols]
     up = rest[:, head_cols : head_cols + width]
     down = rest[:, head_cols + width :]
 
     normed_one, normal_one, inverse_one = norm_forward(inputs, gains[0], biases[0])
-    source_one = gather(normed_one.astype(jnp.bfloat16), "col", 2)
+    source_one = gather(normed_one.astype(jnp.bfloat16), heads_axis, 2)
     qkv_sum = multiply(source_one, qkv_weight, False)
     rows_here = qkv_sum.shape[0]
     qkv_sum = qkv_sum.reshape(rows_here, 3, head_cols)
@@ -228,16 +241,16 @@
     values_all = (qkv_sum[:, 2] + qv_bias[1]).astype(jnp.bfloat16).reshape(shape_four)
     attended, log_sums = attention_forward(queries, keys_all, values_all)
     attended_low = attended.reshape(rows_here, head_cols).astype(jnp.bfloat16)
-    middle = inputs + scatter_sum(multiply(attended_low, out_t, True), "col", 3) + biases[2]
+    middle = inputs + scatter_sum(multiply(attended_low, out_t, True), heads_axis, 3) + biases[2]
     normed_two, normal_two, inverse_two = norm_forward(middle, gains[1], biases[1])
-    source_two = gather(normed_two.astype(jnp.bfloat16), "col", 4)
-    cot_all = gather_async(cot, "col")
+    source_two = gather(normed_two.astype(jnp.bfloat16), heads_axis, 4)
+    cot_all = gather_async(cot, heads_axis)
     before = multiply(source_two, up, False) + up_bias
     hidden_low = gelu_tanh(before).astype(jnp.bfloat16)
     grad_hidden = multiply(cot_all, down, False)
     grad_before = jax.vjp(gelu_tanh, before)[1](grad_hidden)[0].astype(jnp.bfloat16)
-    grad_normed_two = scatter_sum(multiply(grad_before, up, True), "col", 5)
-    output = middle + scatter_sum_async(multiply(hidden_low, down, True), "col") + biases[3]
+    grad_normed_two = scatter_sum(multiply(grad_before, up, True), heads_axis, 5)
+    output = middle + scatter_sum_async(multiply(hidden_low, down, True), heads_axis) + biases[3]
     grad_w_down = contract_tokens(cot_all, hidden_low)
     grad_up_bias = jnp.sum(grad_before.astype(jnp.float32), axis=0)
     grad_w_up = contract_tokens(source_two, grad_before)
@@ -249,7 +262,7 @@
     grad_middle_low = grad_middle.astype(jnp.bfloat16)
     grad_out_bias = jnp.sum(grad_middle_low.astype(jnp.float32), axis=0)
     grad_down_bias = jnp.sum(grad_out, axis=0)
-    grad_middle_all = gather(grad_middle_low, "col", 6)
+    grad_middle_all = gather(grad_middle_low, heads_axis, 6)
     grad_att_low = multiply(grad_middle_all, out_t, False).astype(jnp.bfloat16).reshape(shape_four)
     grad_w_out_t = contract_tokens(grad_middle_all, attended_low)
     grad_q, grad_k, grad_v = attention_backward(
@@ -262,18 +275,18 @@
     grad_qv = jnp.stack(
         [jnp.sum(grad_q.astype(jnp.float32), axis=0), jnp.sum(grad_v.astype(jnp.float32), axis=0)]
     )
-    grad_normed_one = scatter_sum(multiply(grad_qkv_low, qkv_weight, True), "col", 7)
+    grad_normed_one = scatter_sum(multiply(grad_qkv_low, qkv_weight, True), heads_axis, 7)
     grad_w_qkv = contract_tokens(source_one, grad_qkv_low)
     back_one, gain_one, shift_one = norm_backward(
         grad_normed_one, gains[0], normal_one, inverse_one
     )
     grad_input = grad_middle + back_one
 
-    mlp_sum = scatter_sum_async(jnp.concatenate([grad_w_up, grad_w_down], axis=1), "row")
-    mlp_sum = lax.psum(mlp_sum.astype(jnp.bfloat16), "dp").astype(jnp.float32)
-    att_sum = scatter_sum(jnp.concatenate([grad_w_qkv, grad_w_out_t], axis=1), "row", 8)
+    mlp_sum = scatter_sum_async(jnp.concatenate([grad_w_up, grad_w_down], axis=1), split_axis)
+    mlp_sum = flip(lax.psum(mlp_sum.astype(jnp.bfloat16), "dp")).astype(jnp.float32)
+    att_sum = scatter_sum(jnp.concatenate([grad_w_qkv, grad_w_out_t], axis=1), split_axis, 8)
     att_sum = jnp.sum(
-        swap(att_sum.astype(jnp.bfloat16), "dp", True, 9).astype(jnp.float32), axis=0
+        swap(flip(att_sum.astype(jnp.bfloat16)), "dp", True, 9).astype(jnp.float32), axis=0
     )
     sum_up = mlp_sum[:, :width]
     sum_down = mlp_sum[:, width:]
@@ -285,12 +298,13 @@
     small = small + [grad_up_bias, grad_qv.reshape(-1)]
     small = jnp.stack([jnp.pad(row, (0, longest - row.shape[0])) for row in small])
     small = jnp.sum(swap(small, "dp", True, 10), axis=0)
-    small = jnp.sum(swap(small, "row", True, 11), axis=0)
-    sum_upb = small[6, :width]
-    sum_qv = small[7, : 2 * head_cols].reshape(2, head_cols)
+    small = jnp.sum(swap(small, split_axis, True, 11), axis=0)
+    projected = flip(small[6:])
+    sum_upb = projected[0, :width]
+    sum_qv = projected[1, : 2 * head_cols].reshape(2, head_cols)
     share = norm_gains.shape[1]
-    small = lax.dynamic_slice_in_dim(small[:6], lax.axis_index("row") * share, share, axis=1)
-    small = jnp.sum(swap(small, "col", True, 12), axis=0)
+    small = jnp.sum(swap(small[:6], heads_axis, True, 12), axis=0)
+    small = lax.dynamic_slice_in_dim(small, lax.axis_index("row") * share, share, axis=1)
     output_t, grad_input_t = to_features(
         output.astype(jnp.bfloat16), grad_input.astype(jnp.bfloat16), 13
     )

time: 569 us -> 512 us (0.90)
  Pallas kernels: 368 us -> 206 us
  waiting for transfers between devices: 10.6 us -> 91.2 us
  local copies, waits for them, and re-layouts: 48.6 us -> 60.1 us
  starting transfers between devices: 22.2 us -> 29 us
    pallas_call x14, Pallas kernels: 368 us -> 206 us  [swap(): pl.pallas_call(functools.partial(swap_kernel, axis_name, count, shared),...]
    ppermute x2 -> x7, waiting for transfers between devices: 10.5 us -> 90.2 us  [flip(): return lax.ppermute(block, ('row', 'col'), moves)]
    ppermute x2 -> x7, starting transfers between devices: 13.6 us -> 28.4 us  [flip(): return lax.ppermute(block, ('row', 'col'), moves)]
    psum x1, starting transfers between devices: 8.17 us -> 0.25 us  [body(): lax.psum(mlp_sum.astype(jnp.bfloat16), 'dp')]
    unnamed x124 -> x116, local copies, waits for them, and re-layouts: 18.7 us -> 21.4 us
  transfers between devices with their start and end apart: 7 -> 12, of which waited for: 1 -> 3; matrix products, arithmetic and copies ran while one was open for 21% -> 26% of each run, Pallas kernels for 63% -> 41%
where the time goes in v3:
time: 512 us; the launch traced here: 507 us
  Pallas kernels  206 us (40%)
  waiting for transfers between devices  91.2 us (18%)
  local copies, waits for them, and re-layouts  60.1 us (12%)
  matrix products  49.8 us (10%)
  other arithmetic  34.2 us (7%)
  starting transfers between devices  29 us (6%)
  blocking collectives  20.9 us (4%)
  between operations  15.1 us (3%)
    pallas_call x14, Pallas kernels, swap(): pl.pallas_call(functools.partial(swap_kernel, axis_name, count, shared),...  206 us
    ppermute x7, waiting for transfers between devices, flip(): return lax.ppermute(block, ('row', 'col'), moves)  90.2 us
    ppermute x7, starting transfers between devices, flip(): return lax.ppermute(block, ('row', 'col'), moves)  28.4 us
    unnamed x116, local copies, waits for them, and re-layouts  21.4 us
    all_gather x1, blocking collectives, gather_async(): return lax.all_gather(local, axis_name, axis=0, tiled=True)  20.9 us
    dot_general x4, matrix products, multiply(): lax.dot_general(rows, weight, (((1,), (1,)), ((), ())), preferred_element...  15.6 us
    dot_general x4, matrix products, multiply(): return jnp.dot(rows, weight, preferred_element_type=jnp.float32)  15.3 us
  transfers between devices with their start and end apart: 12, of which 3 were waited for; matrix products, arithmetic and copies ran while one was open for 26% of the time, Pallas kernels for 41%

profile of v3, /device:TPU:2, one launch (start us, length us, event | category | flops | bytes accessed | tf_op | source)
XLA Modules:
  0.0 506.5 jit_solution(17390535833920286448)
XLA Ops:
  8.3 1.5 concatenate.46
  9.8 3.5 collective-permute-start.2
  13.3 58.9 %collective-permute-done.2 = bf16[192,1728]{1,0:T(8,128)(2,1)S(1)} collective-permute-done((bf16[192,1728]{1,0:T(8,128)(2,1)S(1)}, bf16[192,1728]{1,0:T(8,128)(2,1)S(1)}, u32[]{:S(2)}, u32[]{:S(2)}) %collective-permute-start.2) | collective-permute-done | bytes 663584 | tf_op jit(solution)/shard_map/ppermute | solution.py:144
  74.3 1.9 collective-permute-start
  76.2 4.8 collective-permute-start.1
  81.0 1.9 collective-permute-start.3
  84.2 12.6 %shard_map.177 = bf16[4,256,384]{2,1,0:T(8,128)(2,1)} custom-call(bf16[4,256,384]{2,1,0:T(8,128)(2,1)} %bitcast.218), custom_call_target="tpu_custom_call" | custom-call | bytes 15728640 | tf_op jit(solution)/shard_map/pallas_call | solution.py:71
  96.8 1.5 slice_bitcast_fusion.4
  98.4 1.5 convert_reduce_fusion.8
  101.2 6.0 %shard_map.178 = f32[4,6,192]{2,1,0:T(8,128)} custom-call(f32[6,192]{1,0:T(8,128)} %pad_maximum_fusion.6.x_ref), custom_call_target="tpu_custom_call" | custom-call | bytes 276480 | tf_op jit(solution)/shard_map/pallas_call | solution.py:71
  109.7 20.9 %shard_map.179 = bf16[4,256,768]{2,1,0:T(8,128)(2,1)} custom-call(bf16[256,768]{1,0:T(8,128)(2,1)} %fusion.70.x_ref), custom_call_target="tpu_custom_call" | custom-call | bytes 23592960 | tf_op jit(solution)/shard_map/pallas_call | solution.py:71
  132.1 20.9 %all_gather.9 = bf16[768,576]{1,0:T(8,128)(2,1)S(1)} all-gather(bf16[192,576]{1,0:T(8,128)(2,1)S(1)} %copy.69), channel_id=1, replica_groups=mesh['dp'=2,'row'=4,'col'=4] {'col'}, dimensions={0}, use_global_device_ids=true | all-gather | bytes 1105920 | tf_op jit(solution)/shard_map/all_gather | solution.py:89
  153.0 1.3 copy.70
  154.3 2.3 fusion.91
  157.9 2.7 squeeze.78
  160.7 1.6 squeeze.79
  162.6 1.7 fusion.79
  165.0 6.7 %while.26 = (s32[]{:T(128)}, bf16[2,512,3,64]{1,3,2,0:T(8,128)(2,1)}, f32[2,3,512]{2,1,0:T(4,128)S(1)}, bf16[2,512,3,64]{1,3,2,0:T(8,128)(2,1)S(1)}, bf16[2,512,...) while((s32[]{:T(128)}, bf16[2,512,3,64]{1,3,2,0:T(8,128)(2,1)}, ...), condition=%wide.region_5.6_spmd, body=%wide.region_2.5_spmd.sunk | while | flops 211024384 | bytes 11530321 | solution.py:184
  166.6 1.8 fusion.127
  170.0 1.8 fusion.127
  171.8 1.5 copy.74
  174.2 2.9 convolution_convert_fusion.3
  177.1 20.3 %shard_map.180 = bf16[4,256,768]{2,1,0:T(8,128)(2,1)} custom-call(bf16[4,256,768]{2,1,0:T(8,128)(2,1)} %bitcast.212), custom_call_target="tpu_custom_call" | custom-call | bytes 31457280 | tf_op jit(solution)/shard_map/pallas_call | solution.py:71
  197.4 1.7 convert_reduce_fusion.5
  201.8 20.8 %shard_map.181 = bf16[4,256,768]{2,1,0:T(8,128)(2,1)} custom-call(bf16[256,768]{1,0:T(8,128)(2,1)} %add_convert_fusion.1.x_ref), custom_call_target="tpu_custom_call" | custom-call | bytes 23592960 | tf_op jit(solution)/shard_map/pallas_call | solution.py:71
  222.6 3.3 fusion.61
  225.9 1.6 copy-done.51
  227.6 4.8 convolution_convert_fusion.2
  232.6 1.7 copy.83
  235.6 2.0 reshape.193
  237.6 7.5 %convert_reduce_fusion.4 = (f32[768]{0:T(1024)}, bf16[1024,768]{1,0:T(8,128)(2,1)S(1)}) fusion(bf16[1024,768]{1,0:T(8,128)(2,1)} %all-gather.5.cloned.1.call-done, bf16[768,1728]{1,0:T(8,128)(2,1)} %all-gather.3.cloned.1.call-done, f32[1024,768]{1,0:T(8,128)} %copy-done.51, f32[768]{0:T(1024)} %collective-permute-done.3), kind=kOutput, calls=%fused_computation.70 | convolution fusion | flops 1229192448 | bytes 7478272 | tf_op jit(solution)/shard_map/dot_general | solution.py:30
  246.3 1.4 convolution_convert_fusion.5
  248.8 2.7 convolution_convert_fusion.4
  251.4 1.6 pad_maximum_fusion
  253.0 4.4 copy.93
  257.4 4.0 convolution_convert_fusion.1
  261.5 21.3 %shard_map.182 = bf16[4,256,768]{2,1,0:T(8,128)(2,1)} custom-call(bf16[4,256,768]{2,1,0:T(8,128)(2,1)} %bitcast.223), custom_call_target="tpu_custom_call" | custom-call | bytes 31457280 | tf_op jit(solution)/shard_map/pallas_call | solution.py:71
  282.8 2.1 convert_reduce_fusion.2
  286.4 2.7 multiply_reduce_fusion.1
  289.1 1.9 convert_reduce_fusion.11
  291.0 20.8 %shard_map.183 = bf16[4,256,768]{2,1,0:T(8,128)(2,1)} custom-call(bf16[256,768]{1,0:T(8,128)(2,1)} %get-tuple-element.223.x_ref), custom_call_target="tpu_custom_call" | custom-call | bytes 23592960 | tf_op jit(solution)/shard_map/pallas_call | solution.py:71
  311.9 2.2 convolution_convert_fusion.8
  316.7 11.5 %while.27 = (s32[]{:T(128)}, bf16[2,512,3,64]{1,3,2,0:T(8,128)(2,1)}, bf16[2,512,3,64]{1,3,2,0:T(8,128)(2,1)}, bf16[2,512,3,64]{1,3,2,0:T(8,128)(2,1)}, bf16[2,5...) while((s32[]{:T(128)}, ...), condition=%wide.region_15.16_spmd, body=%wide.region_13.15_spmd.sunk | while | flops 510851584 | bytes 33002712 | solution.py:211
  328.2 1.6 copy.84
  330.8 1.5 copy.80
  334.1 1.4 convolution_convert_fusion.6
  336.8 23.2 %shard_map.189 = bf16[4,192,768]{2,1,0:T(8,128)(2,1)} custom-call(bf16[4,192,768]{2,1,0:T(8,128)(2,1)} %pad_maximum_fusion.1.x_ref), custom_call_target="tpu_custom_call" | custom-call | bytes 23592960 | tf_op jit(solution)/shard_map/pallas_call | solution.py:71
  360.0 2.2 reduce_sum.269
  362.3 10.0 %collective-permute-start.4 = (bf16[192,768]{1,0:T(8,128)(2,1)}, bf16[192,768]{1,0:T(8,128)(2,1)S(1)}, u32[]{:S(2)}, u32[]{:S(2)}) collective-permute-start(bf16[192,768]{1,0:T(8,128)(2,1)} %reduce_sum.269), channel_id=1, source_target_pairs={{0,0},{1,4},{2,8},{3,12},{4,1},{5,5},{6,9},{7,13},{8,2},{9,6},{10,... | collective-permute-start | bytes 884744 | tf_op jit(solution)/shard_map/ppermute | solution.py:144
  373.8 3.9 convolution_convert_fusion
  377.8 22.3 %shard_map.184 = bf16[4,256,768]{2,1,0:T(8,128)(2,1)} custom-call(bf16[4,256,768]{2,1,0:T(8,128)(2,1)} %bitcast.222), custom_call_target="tpu_custom_call" | custom-call | bytes 31457280 | tf_op jit(solution)/shard_map/pallas_call | solution.py:71
  400.1 2.1 convert_reduce_fusion
  403.5 2.6 shard_map.186
  406.1 1.4 reduce_sum.266.x_ref
  407.5 9.8 %shard_map.187 = f32[4,8,768]{2,1,0:T(8,128)} custom-call(f32[8,768]{1,0:T(8,128)} %reduce_sum.266.x_ref), custom_call_target="tpu_custom_call" | custom-call | bytes 1474560 | tf_op jit(solution)/shard_map/pallas_call | solution.py:71
  418.8 8.9 %shard_map.188 = f32[4,6,768]{2,1,0:T(8,128)} custom-call(f32[6,768]{1,0:T(8,128)} %bitcast.240), custom_call_target="tpu_custom_call" | custom-call | bytes 1105920 | tf_op jit(solution)/shard_map/pallas_call | solution.py:71
  427.7 2.9 collective-permute-start.5
  431.6 2.2 copy.94
  435.0 13.1 %shard_map.185 = bf16[4,256,384]{2,1,0:T(8,128)(2,1)} custom-call(bf16[4,256,384]{2,1,0:T(8,128)(2,1)} %pad_maximum_fusion.3.x_ref), custom_call_target="tpu_custom_call" | custom-call | bytes 15728640 | tf_op jit(solution)/shard_map/pallas_call | solution.py:71
  448.1 1.5 fusion.87
  453.7 1.4 copy.86
  455.1 3.4 collective-permute-start.6
  460.5 3.4 shard_map.190
  467.3 31.3 %collective-permute-done.6 = bf16[192,1536]{1,0:T(8,128)(2,1)S(1)} collective-permute-done((bf16[192,1536]{1,0:T(8,128)(2,1)S(1)}, bf16[192,1536]{1,0:T(8,128)(2,1)S(1)}, u32[]{:S(2)}, u32[]{:S(2)}) %collective-permute-start.6) | collective-permute-done | bytes 589856 | tf_op jit(solution)/shard_map/ppermute | solution.py:144
  (251 shorter events, 58.6 us)
Async XLA Ops:
  7.2 75.8 %copy-start.23 = (bf16[192,1024]{1,0:T(8,128)(2,1)S(1)}, bf16[192,1024]{1,0:T(8,128)(2,1)}, u32[]{:S(2)}) copy-start(bf16[192,1024]{1,0:T(8,128)(2,1)} %param.14) | copy-start | bytes 1179652
  7.2 75.8 %copy-start.22 = (bf16[192,1024]{1,0:T(8,128)(2,1)S(1)}, bf16[192,1024]{1,0:T(8,128)(2,1)}, u32[]{:S(2)}) copy-start(bf16[192,1024]{1,0:T(8,128)(2,1)} %param.23) | copy-start | bytes 1179652
  7.2 167.0 %all-gather.3.cloned.1.call-start = ((), (), s32[]{:S(2)}) async-start(), calls=%async_computation.2 | async-start | bytes 3440640 | tf_op jit(solution)/shard_map/all_gather | solution.py:89
  9.8 62.4 %collective-permute-start.2 = (bf16[192,1728]{1,0:T(8,128)(2,1)S(1)}, bf16[192,1728]{1,0:T(8,128)(2,1)S(1)}, u32[]{:S(2)}, u32[]{:S(2)}) collective-permute-start(bf16[192,1728]{1,0:T(8,128)(2,1)S(1)} %concatenate.46), channel_id=1, source_target_pairs={{0,0},{1,4},{2,8},{3,12},{4,1},{5,5},{6,9},{7,13},{8,2},{9,6},{10,... | collective-permute-start | bytes 1990664 | tf_op jit(solution)/shard_map/ppermute | solution.py:144
  73.1 164.5 %all-gather.5.cloned.1.call-start = ((), (), s32[]{:S(2)}) async-start(), calls=%async_computation.4 | async-start | bytes 1966080 | tf_op jit(solution)/shard_map/all_gather | solution.py:89
  74.3 56.5 %collective-permute-start = (bf16[192,576]{0,1:T(8,128)(2,1)S(1)}, bf16[192,576]{0,1:T(8,128)(2,1)}, u32[]{:S(2)}, u32[]{:S(2)}) collective-permute-start(bf16[192,576]{0,1:T(8,128)(2,1)S(1)} %bitcast.239), channel_id=1, source_target_pairs={{0,0},{1,4},{2,8},{3,12},{4,1},{5,5},{6,9},{7,13},{8,2},{9,6},{10,... | collective-permute-start | bytes 663560 | tf_op jit(solution)/shard_map/ppermute | solution.py:144
  76.2 54.4 %collective-permute-start.1 = (f32[2,192]{1,0:T(2,128)}, f32[2,192]{1,0:T(2,128)S(1)}, u32[]{:S(2)}, u32[]{:S(2)}) collective-permute-start(f32[2,192]{1,0:T(2,128)} %param.18), channel_id=1, source_target_pairs={{0,0},{1,4},{2,8},{3,12},{4,1},{5,5},{6,9},{7,13},{8,2},{9,6},{10,... | collective-permute-start | bytes 4616 | tf_op jit(solution)/shard_map/ppermute | solution.py:144
  81.0 144.9 %collective-permute-start.3 = (f32[768]{0:T(1024)}, f32[768]{0:T(1024)}, u32[]{:S(2)}, u32[]{:S(2)}) collective-permute-start(f32[768]{0:T(1024)} %param.21), channel_id=1, source_target_pairs={{0,0},{1,4},{2,8},{3,12},{4,1},{5,5},{6,9},{7,13},{8,2},{9,6},{10,... | collective-permute-start | bytes 9224 | tf_op jit(solution)/shard_map/ppermute | solution.py:144
  96.8 3.7 copy-start.47
  96.8 3.7 copy-start.49
  99.9 186.4 %reduce-scatter.5.cloned.1.call-start = ((), (), s32[]{:S(2)}) async-start(), calls=%async_computation.3 | async-start | bytes 1966080 | tf_op jit(solution)/shard_map/reduce_scatter | solution.py:93
  100.3 30.6 %copy-start.32 = (f32[256]{0:T(256)}, f32[256]{0:T(256)S(1)}, u32[]{:S(2)}) copy-start(f32[256]{0:T(256)S(1)} %broadcast_multiply_fusion.5) | copy-start | bytes 3076
  100.5 30.3 %copy-start.36 = (f32[256]{0:T(256)}, f32[256]{0:T(256)S(1)}, u32[]{:S(2)}) copy-start(f32[256]{0:T(256)S(1)} %add_rsqrt_fusion.1) | copy-start | bytes 3076
  108.0 1.0 copy-start.28
  130.6 23.7 %copy-start.1 = (bf16[4,256,768]{2,1,0:T(8,128)(2,1)S(1)}, bf16[4,256,768]{2,1,0:T(8,128)(2,1)}, u32[]{:S(2)}) copy-start(bf16[4,256,768]{2,1,0:T(8,128)(2,1)} %shard_map.179) | copy-start | bytes 4718596
  153.0 3.6 copy-start.4
  157.9 2.8 copy-start.11
  171.8 25.6 %copy-start.2 = (bf16[2,512,3,64]{1,3,2,0:T(8,128)(2,1)}, bf16[2,512,3,64]{1,3,2,0:T(8,128)(2,1)S(1)}, u32[]{:S(2)}) copy-start(bf16[2,512,3,64]{1,3,2,0:T(8,128)(2,1)S(1)} %get-tuple-element.424) | copy-start | bytes 1179652
  173.3 24.1 %copy-start.7 = (bf16[2,512,3,64]{1,0,3,2:T(2,128)(2,1)}, bf16[2,512,3,64]{1,0,3,2:T(2,128)(2,1)S(1)}, u32[]{:S(2)}) copy-start(bf16[2,512,3,64]{1,0,3,2:T(2,128)(2,1)S(1)} %copy.74) | copy-start | bytes 1179652
  197.4 3.4 copy-start.30
  197.4 3.4 copy-start.41
  225.9 1.7 copy-start.51
  232.4 199.2 %reduce-scatter.7.cloned.1.call-start = ((), (), s32[]{:S(2)}) async-start(), calls=%async_computation.6 | async-start | bytes 2949120
  237.6 8.7 %copy-start.19 = (bf16[4,256,768]{2,1,0:T(8,128)(2,1)S(1)}, bf16[4,256,768]{2,1,0:T(8,128)(2,1)}, u32[]{:S(2)}) copy-start(bf16[4,256,768]{2,1,0:T(8,128)(2,1)} %shard_map.181) | copy-start | bytes 4718596
  245.1 1.2 copy-start.53
  246.3 1.4 copy-start.50
  246.3 2.4 copy-start.52
  253.0 4.4 copy-start.54
  261.5 24.0 %copy-start.48 = (f32[768]{0:T(1024)S(1)}, f32[768]{0:T(1024)}, u32[]{:S(2)}) copy-start(f32[768]{0:T(1024)} %get-tuple-element.260) | copy-start | bytes 9220
  282.8 3.6 copy-start.31
  282.8 3.6 copy-start.35
  282.8 3.6 copy-start.39
  282.8 3.6 copy-start.40
  284.9 4.2 copy-start.6
  286.1 167.6 %all-reduce.3.cloned.1.call-start = ((), (), s32[]{:S(2)}) async-start(), calls=%async_computation.5 | async-start | bytes 1572864 | tf_op jit(solution)/shard_map/psum | solution.py:286
  311.8 4.9 copy-start.3
  316.7 11.5 %copy-start = (bf16[4,256,768]{2,1,0:T(8,128)(2,1)S(1)}, bf16[4,256,768]{2,1,0:T(8,128)(2,1)}, u32[]{:S(2)}) copy-start(bf16[4,256,768]{2,1,0:T(8,128)(2,1)} %shard_map.183) | copy-start | bytes 4718596
  318.4 1.0 copy-start.16
  318.4 1.6 copy-start.8
  320.0 1.2 copy-start.17
  324.1 1.0 copy-start.16
  324.2 1.6 copy-start.8
  325.7 1.2 copy-start.17
  328.2 1.6 copy-start.10
  328.2 2.1 copy-start.18
  330.3 2.2 copy-start.15
  330.3 2.2 copy-start.21
  332.3 1.9 copy-start.14
  332.5 3.1 copy-start.26
  336.8 37.0 %copy-start.5 = (bf16[768,576]{1,0:T(8,128)(2,1)S(1)}, bf16[768,576]{1,0:T(8,128)(2,1)}, u32[]{:S(2)}) copy-start(bf16[768,576]{1,0:T(8,128)(2,1)} %copy-done.4) | copy-start | bytes 2654212
  362.3 97.5 %collective-permute-start.4 = (bf16[192,768]{1,0:T(8,128)(2,1)}, bf16[192,768]{1,0:T(8,128)(2,1)S(1)}, u32[]{:S(2)}, u32[]{:S(2)}) collective-permute-start(bf16[192,768]{1,0:T(8,128)(2,1)} %reduce_sum.269), channel_id=1, source_target_pairs={{0,0},{1,4},{2,8},{3,12},{4,1},{5,5},{6,9},{7,13},{8,2},{9,6},{10,... | collective-permute-start | bytes 884744 | tf_op jit(solution)/shard_map/ppermute | solution.py:144
  377.7 24.5 %copy-start.29 = (f32[768]{0:T(1024)S(1)}, f32[768]{0:T(1024)}, u32[]{:S(2)}) copy-start(f32[768]{0:T(1024)} %copy-done.28) | copy-start | bytes 9220
  377.7 24.6 %copy-start.33 = (f32[256]{0:T(256)S(1)}, f32[256]{0:T(256)}, u32[]{:S(2)}) copy-start(f32[256]{0:T(256)} %copy-done.32) | copy-start | bytes 3076
  377.7 24.6 %copy-start.37 = (f32[256]{0:T(256)S(1)}, f32[256]{0:T(256)}, u32[]{:S(2)}) copy-start(f32[256]{0:T(256)} %copy-done.36) | copy-start | bytes 3076
  377.7 25.0 %copy-start.43 = (f32[768]{0:T(1024)S(1)}, f32[768]{0:T(1024)}, u32[]{:S(2)}) copy-start(f32[768]{0:T(1024)} %get-tuple-element.222) | copy-start | bytes 9220
  377.7 25.0 %copy-start.42 = (f32[768]{0:T(1024)S(1)}, f32[768]{0:T(1024)}, u32[]{:S(2)}) copy-start(f32[768]{0:T(1024)} %get-tuple-element.172) | copy-start | bytes 9220
  377.8 25.0 %copy-start.44 = (f32[1,768]{1,0:T(1,128)S(1)}, f32[1,768]{1,0:T(1,128)}, u32[]{:S(2)}) copy-start(f32[1,768]{1,0:T(1,128)} %stack.61) | copy-start | bytes 9220
  377.8 25.0 %copy-start.45 = (f32[1,768]{1,0:T(1,128)S(1)}, f32[1,768]{1,0:T(1,128)}, u32[]{:S(2)}) copy-start(f32[1,768]{1,0:T(1,128)} %stack.59) | copy-start | bytes 9220
  377.8 25.0 %copy-start.46 = (f32[1,768]{1,0:T(1,128)S(1)}, f32[1,768]{1,0:T(1,128)}, u32[]{:S(2)}) copy-start(f32[1,768]{1,0:T(1,128)} %stack.62) | copy-start | bytes 9220
  400.1 30.4 %copy-start.12 = (f32[256,768]{1,0:T(8,128)S(1)}, f32[256,768]{1,0:T(8,128)}, u32[]{:S(2)}) copy-start(f32[256,768]{1,0:T(8,128)} %get-tuple-element.224) | copy-start | bytes 2359300
  402.3 28.8 %copy-start.13 = (bf16[256,768]{1,0:T(8,128)(2,1)S(1)}, bf16[256,768]{1,0:T(8,128)(2,1)}, u32[]{:S(2)}) copy-start(bf16[256,768]{1,0:T(8,128)(2,1)} %get-tuple-element.237) | copy-start | bytes 1179652
  427.7 30.8 %collective-permute-start.5 = (f32[2,768]{1,0:T(2,128)S(1)}, f32[2,768]{1,0:T(2,128)S(1)}, u32[]{:S(2)}, u32[]{:S(2)}) collective-permute-start(f32[2,768]{1,0:T(2,128)S(1)} %slice.215), channel_id=1, source_target_pairs={{0,0},{1,4},{2,8},{3,12},{4,1},{5,5},{6,9},{7,13},{8,2},{9,6},{10,... | collective-permute-start | bytes 18440 | tf_op jit(solution)/shard_map/ppermute | solution.py:144
  431.5 16.5 %copy-start.24 = (f32[4,6,768]{2,1,0:T(8,128)S(1)}, f32[4,6,768]{2,1,0:T(8,128)}, u32[]{:S(2)}) copy-start(f32[4,6,768]{2,1,0:T(8,128)} %shard_map.188) | copy-start | bytes 221188
  455.1 43.6 %collective-permute-start.6 = (bf16[192,1536]{1,0:T(8,128)(2,1)S(1)}, bf16[192,1536]{1,0:T(8,128)(2,1)S(1)}, u32[]{:S(2)}, u32[]{:S(2)}) collective-permute-start(bf16[192,1536]{1,0:T(8,128)(2,1)S(1)} %copy.86), channel_id=1, source_target_pairs={{0,0},{1,4},{2,8},{3,12},{4,1},{5,5},{6,9},{7,13},{8,2},{9,6},{10,... | collective-permute-start | bytes 1769480 | tf_op jit(solution)/shard_map/ppermute | solution.py:144
  (7 other events, 4.8 us)
Sparse Core Ops, SparseCore 0:
  73.2 57.2 all-gather.2
  132.9 30.5 all-gather.4
  232.5 30.3 reduce-scatter.4
  286.2 46.6 reduce-scatter.6
  434.0 19.6 all-reduce.2
